TPU v7x, 32 devices: a whole 2x2x4 slice. The times are simulated.
32 devices in a mesh: ctx: 8 (over z, core), tp: 4 (over y, x).
Axes of the slice: x: 2, y: 2, z: 4, core: 2. Of those that a mesh axis runs over, the one named last changes fastest.
Arguments:
- tokens: bfloat16 [4096, 8192], P(('ctx', 'tp')), may hold values from -6 to 6
- norm_gain: float32 [8192], replicated, may hold values from 0.1 to 1.9
- w_query: bfloat16 [8192, 4096], P(None, 'tp'), may hold values from -1 to 1
- query_scale: float32 [64, 32], P(None, 'tp'), may hold values from 0.5 to 2
- w_key: bfloat16 [8192, 1024], P(None, 'tp'), may hold values from -1 to 1
- key_scale: float32 [64, 8], P(None, 'tp'), may hold values from 0.5 to 2
- w_value: bfloat16 [8192, 1024], P(None, 'tp'), may hold values from -0.0625 to 0.0625
- value_scale: float32 [64, 8], P(None, 'tp'), may hold values from 0.5 to 2
- w_out: bfloat16 [4096, 8192], P('tp'), may hold values from -0.09375 to 0.09375
- out_scale: float32 [32, 64], P('tp'), may hold values from 0.5 to 2
- score_vec: bfloat16 [8192], replicated, may hold values from -0.0625 to 0.0625
- doc_ids: int32 [4096], replicated, may hold values from 0 to 3, never falling along the last dimension, each value on 1 to 1280 neighbouring positions
- span_of: int32 [8], replicated, may hold values from 0 to 7, each once
Outputs:
- hidden: bfloat16 [4096, 8192], P(('ctx', 'tp'))
- doc_score: float32 [4], replicated
Inputs may be any that keep to these rules, and one draw needn't show every extreme that they name: `doc_ids`: document numbers never fall along the stream; every document has 1 to 1280 tokens and one has exactly 1280. `span_of`: each span is held by exactly one index of ctx.
All inputs are finite; a program needn't handle non-finite values.
Results may differ from a plain program's by a relative error of at most 0.012.
The roundings to bfloat16 on the way count: a program that leaves them out, or rounds other values in their place, can miss the bound.
Values may be sent and summed in bfloat16 or wider, within the bound.
No kernel may reach another device: no remote copies, remote signals or barrier semaphores. Data moves between devices by JAX's collectives and lax.ppermute only.
A program may use at most 192 MiB of HBM per device.

v0:
```python
import jax
import jax.numpy as jnp
from jax import lax
from jax.sharding import PartitionSpec as P

HDIM = 128
BLOCK = 128
NDOC = 4


def rms_norm(values_in, gain):
    widened = values_in.astype(jnp.float32)
    factor = lax.rsqrt(jnp.mean(widened * widened, -1, keepdims=True) + 1e-05)
    return (widened * factor * gain).astype(jnp.bfloat16)


def dequant(stored, scales):
    expanded = jnp.repeat(jnp.repeat(scales, BLOCK, 0), BLOCK, 1)
    return (stored.astype(jnp.float32) * expanded).astype(jnp.bfloat16)


def rotate(heads_in, positions):
    half_dim = heads_in.shape[-1] // 2
    frequency = 500000.0 ** (-2.0 * jnp.arange(half_dim).astype(jnp.float32) / heads_in.shape[-1])
    angles = positions.astype(jnp.float32)[:, None] * frequency[None, :]
    cosine = jnp.cos(angles)[:, None, :]
    sine = jnp.sin(angles)[:, None, :]
    lower_half = heads_in[..., :half_dim]
    upper_half = heads_in[..., half_dim:]
    return jnp.concatenate(
        [lower_half * cosine - upper_half * sine, upper_half * cosine + lower_half * sine], -1
    )


def attend(state, query_group, key_block, value_block, visible):
    run_max, run_total, run_acc = state
    scores = jnp.einsum(
        "qkgd,nkd->kgqn", query_group, key_block, preferred_element_type=jnp.float32
    ) * HDIM ** (-0.5)
    scores = jnp.where(visible[None, None], scores, -1e30)
    new_max = jnp.maximum(run_max, jnp.max(scores, -1))
    weights = jnp.where(visible[None, None], jnp.exp(scores - new_max[..., None]), 0.0)
    fading = jnp.exp(run_max - new_max)
    new_total = run_total * fading + jnp.sum(weights, -1)
    new_acc = run_acc * fading[..., None] + jnp.einsum(
        "kgqn,nkd->kgqd",
        weights.astype(jnp.bfloat16),
        value_block,
        preferred_element_type=jnp.float32,
    )
    return (new_max, new_total, new_acc)


def on_device(
    tokens,
    norm_gain,
    w_query,
    query_scale,
    w_key,
    key_scale,
    w_value,
    value_scale,
    w_out,
    out_scale,
    score_vec,
    doc_ids,
    span_of,
):
    rows = tokens.shape[0]
    tp_count = lax.axis_size("tp")
    span_len = rows * tp_count
    slot = lax.axis_index("ctx")
    member = lax.axis_index("tp")
    span_pos = span_of[slot]
    doc_iota = jnp.arange(NDOC, dtype=jnp.int32)
    counts = jnp.sum((doc_ids[:, None] == doc_iota[None, :]).astype(jnp.int32), 0)
    starts = jnp.cumsum(counts) - counts
    query_pos = span_pos * span_len + jnp.arange(span_len, dtype=jnp.int32)
    query_doc = jnp.take(doc_ids, query_pos)
    relative = query_pos - jnp.take(starts, query_doc)
    normed = rms_norm(tokens, norm_gain)
    query_cols = w_query.shape[1]
    key_cols = w_key.shape[1]
    w_joint = jnp.concatenate(
        [dequant(w_query, query_scale), dequant(w_key, key_scale), dequant(w_value, value_scale)], 1
    )
    joint = jnp.dot(
        lax.all_gather(normed, "tp", axis=0, tiled=True),
        w_joint,
        preferred_element_type=jnp.float32,
    )
    heads_here = query_cols // HDIM
    kv_here = key_cols // HDIM
    group = heads_here // kv_here
    queries = rotate(joint[:, :query_cols].reshape(span_len, heads_here, HDIM), relative).astype(
        jnp.bfloat16
    )
    queries = queries.reshape(span_len, kv_here, group, HDIM)
    keys = rotate(
        joint[:, query_cols : query_cols + key_cols].reshape(span_len, kv_here, HDIM), relative
    ).astype(jnp.bfloat16)
    values_here = (
        joint[:, query_cols + key_cols :].reshape(span_len, kv_here, HDIM).astype(jnp.bfloat16)
    )
    state = (
        jnp.full((kv_here, group, span_len), -1e30, jnp.float32),
        jnp.zeros((kv_here, group, span_len), jnp.float32),
        jnp.zeros((kv_here, group, span_len, HDIM), jnp.float32),
    )
    local_visible = (query_doc[:, None] == query_doc[None, :]) & (
        query_pos[None, :] <= query_pos[:, None]
    )
    state = attend(state, queries, keys, values_here, local_visible)

    def maybe_attend(inner_state, key_block, value_block, visible):
        return lax.cond(
            jnp.any(visible),
            lambda current: attend(current, queries, key_block, value_block, visible),
            lambda current: current,
            inner_state,
        )

    key_piece = lax.all_gather(keys, "ctx", axis=0, tiled=True)
    value_piece = lax.all_gather(values_here, "ctx", axis=0, tiled=True)
    length = key_piece.shape[0]
    blocks = max(length // span_len, 1)
    block_len = length // blocks

    def one_block(inner_state, block_index):
        offset = block_index * block_len
        key_block = lax.dynamic_slice_in_dim(key_piece, offset, block_len, 0)
        value_block = lax.dynamic_slice_in_dim(value_piece, offset, block_len, 0)
        row_index = offset + jnp.arange(block_len, dtype=jnp.int32)
        source = row_index // span_len
        key_pos = jnp.take(span_of, source) * span_len + row_index % span_len
        key_doc = jnp.take(doc_ids, key_pos)
        visible = (
            (source[None, :] != slot)
            & (query_doc[:, None] == key_doc[None, :])
            & (key_pos[None, :] <= query_pos[:, None])
        )
        return (maybe_attend(inner_state, key_block, value_block, visible), None)

    final_state, unused = lax.scan(one_block, state, jnp.arange(blocks, dtype=jnp.int32))
    state = final_state
    run_max, run_total, run_acc = state
    attended = (
        (run_acc / run_total[..., None])
        .transpose(2, 0, 1, 3)
        .reshape(span_len, query_cols)
        .astype(jnp.bfloat16)
    )
    w_back = dequant(w_out, out_scale)
    mixed = lax.psum_scatter(
        jnp.dot(attended, w_back, preferred_element_type=jnp.float32).astype(jnp.bfloat16),
        "tp",
        scatter_dimension=0,
        tiled=True,
    ).astype(jnp.float32)
    hidden = (tokens.astype(jnp.float32) + mixed).astype(jnp.bfloat16)
    row_score = jnp.dot(hidden, score_vec, preferred_element_type=jnp.float32)
    own_doc = lax.dynamic_slice_in_dim(query_doc, member * rows, rows, 0)
    partial_sums = jnp.sum(
        jnp.where(own_doc[:, None] == doc_iota[None, :], row_score[:, None], 0.0), 0
    )
    totals = lax.psum(partial_sums, ("ctx", "tp"))
    return (hidden, totals / counts.astype(jnp.float32))


def solution(mesh):
    return jax.shard_map(
        on_device,
        mesh=mesh,
        in_specs=(
            P(("ctx", "tp"), None),
            P(),
            P(None, "tp"),
            P(None, "tp"),
            P(None, "tp"),
            P(None, "tp"),
            P(None, "tp"),
            P(None, "tp"),
            P("tp", None),
            P("tp", None),
            P(),
            P(),
            P(),
        ),
        out_specs=(P(("ctx", "tp"), None), P()),
        check_vma=False,
    )
```

profile of v0, /device:TPU:0, one launch (start us, length us, event | category | flops | bytes accessed | tf_op | source)
XLA Modules:
  0.0 516.2 jit_solution(15245598192146823685)
XLA Ops:
  7.3 2.1 fusion.43
  9.4 3.5 fusion.45
  14.2 3.1 gather_fusion.1
  18.7 2.7 and_select_fusion.2
  21.3 1.8 multiply_cosine_fusion
  23.4 18.8 %broadcast_in_dim.144 = f32[8192,2,128]{2,1,0:T(2,128)S(1)} broadcast(f32[8192,2]{1,0:T(8,128)S(1)} %bitcast.143), dimensions={0,1} | broadcast | bytes 8454144 | tf_op jit(solution)/shard_map/broadcast_in_dim | solution.py:18
  42.5 18.8 %broadcast_in_dim.146 = f32[8192,2,128]{2,1,0:T(2,128)S(1)} broadcast(f32[8192,2]{1,0:T(8,128)S(1)} %bitcast.144), dimensions={0,1} | broadcast | bytes 8454144 | tf_op jit(solution)/shard_map/broadcast_in_dim | solution.py:18
  61.3 9.1 %fusion.38 = (bf16[8192,256]{1,0:T(8,128)(2,1)}, bf16[8192,256]{1,0:T(8,128)(2,1)}) fusion(f32[1024,8,2,128]{3,2,1,0:T(2,128)S(1)} %bitcast.141, bf16[8192,256]{1,0:T(8,128)(2,1)} %param.25, f32[1024,8,2,128]{3,2,1,0:T(2,128)S(1)} %bitcast.140, bf16[8192,256]{1,0:T(8,128)(2,1)} %param.23), kind=kLoop, calls=%fused_computation.68 | loop fusion | flops 12582912 | bytes 33554432 | tf_op jit(solution)/shard_map/convert_element_type | solution.py:19
  70.4 2.2 broadcast_in_dim.141
  72.6 10.3 %broadcast_in_dim.142 = f32[8192,8,128]{2,1,0:T(8,128)S(1)} broadcast(f32[8192,8]{1,0:T(8,128)} %bitcast.145), dimensions={0,1} | broadcast | bytes 33816576 | tf_op jit(solution)/shard_map/broadcast_in_dim | solution.py:18
  82.9 18.0 %fusion.26 = bf16[8192,1024]{1,0:T(8,128)(2,1)} fusion(f32[1024,8,8,128]{3,2,1,0:T(8,128)S(1)} %bitcast.139, bf16[8192,1024]{1,0:T(8,128)(2,1)} %param.21), kind=kLoop, calls=%fused_computation.58 | loop fusion | flops 25165824 | bytes 67108864 | tf_op jit(solution)/shard_map/convert_element_type | solution.py:19
  100.9 2.5 all-gather.4.cloned.1.call-done
  103.3 19.8 %fusion.27 = f32[512,1536]{1,0:T(8,128)S(1)} fusion(bf16[512,8192]{1,0:T(8,128)(2,1)} %all-gather.4.cloned.1.call-done, bf16[8192,256]{1,0:T(8,128)(2,1)} %get-tuple-element.374, bf16[8192,256]{1,0:T(8,128)(2,1)} %get-tuple-element.375, bf16[8192,1024]{1,0:T(8,128)(2,1)} %fusion.26), kind=kOutput, calls=%fused_computation.59 | convolution fusion | flops 12960399360 | bytes 36700160 | tf_op jit(solution)/shard_map/dot_general | solution.py:87
  123.2 1.6 copy-done.3
  124.8 0.8 slice.55
  125.6 1.3 reshape.344
  127.6 1.1 subtract_convert_fusion.1
  128.7 0.9 pad_maximum_fusion.1
  129.6 1.8 copy_bitcast_fusion
  131.7 1.1 slice.68
  132.8 1.7 slice_bitcast_fusion
  135.0 0.9 subtract_convert_fusion
  137.5 2.5 fusion.40
  140.1 2.3 fusion.42
  142.4 2.9 fusion.50
  145.3 13.7 %all-gather.6.cloned.1.call-done = bf16[4096,2,128]{2,0,1:T(8,128)(2,1)} async-done(((bf16[512,2,128]{2,0,1:T(8,128)(2,1)}), bf16[4096,2,128]{2,0,1:T(8,128)(2,1)}) %all-gather.6.cloned.1.call-update) | async-done | bytes 2097168 | tf_op jit(solution)/shard_map/all_gather | solution.py:123
  159.1 30.2 %all-gather.8.cloned.1.call-done = bf16[4096,2,128]{2,0,1:T(8,128)(2,1)} async-done(((bf16[512,2,128]{2,0,1:T(8,128)(2,1)}), bf16[4096,2,128]{2,0,1:T(8,128)(2,1)}) %all-gather.8.cloned.1.call-update) | async-done | bytes 2097168 | tf_op jit(solution)/shard_map/all_gather | solution.py:124
  189.3 104.2 %while.17 = (s32[]{:T(128)}, f32[2,4,512]{2,1,0:T(4,128)S(1)}, f32[2,4,512]{2,1,0:T(4,128)S(1)}, f32[2,4,512,128]{3,2,1,0:T(8,128)S(1)}, s32[8]{0:T(128)S(1)}, /...) while((s32[]{:T(128)}, f32[2,4,512]{2,1,0:T(4,128)S(1)}, ...), condition=%wide.region_11.13_spmd.clone, body=%wide.region_5.0_spmd.clone.sunk | while | flops 1103429120 | bytes 32283076 | solution.py:144
  191.2 4.3 compare_select_fusion.16
  196.3 3.1 gather_fusion
  199.4 1.1 fusion.77
  203.1 4.3 compare_select_fusion.16
  208.1 3.1 gather_fusion
  211.3 1.1 fusion.77
  215.0 4.3 compare_select_fusion.16
  220.0 3.1 gather_fusion
  223.2 1.1 fusion.77
  224.9 9.1 %conditional.3 = ((f32[2,4,512]{2,1,0:T(4,128)S(1)}, f32[2,4,512]{2,1,0:T(4,128)S(1)}, f32[2,4,512,128]{3,2,1,0:T(8,128)S(1)})) conditional(s32[]{:T(128)} %convert_element_type.157, (f32[2,4,512]{2,1,0:T(4,128)S(1)}, f32[2,4,512]{2,1,0:T(4,128)S(1)}, f32[2,4,512,128]{3,2,1,0:T(8,128)S(1)}) %tuple.85, (pred[512,512]{0,1:T(8,128)(4,1)S(1)}, ...), branch_computations={%region_7.8_spmd, %region_8.11_spmd} | conditional | flops 1102061568 | bytes 31981642 | solution.py:116
  224.9 2.5 fusion.2
  227.5 2.0 fusion.4
  229.6 4.5 multiply_add_fusion
  236.0 4.3 compare_select_fusion.16
  241.0 3.1 gather_fusion
  244.2 1.1 fusion.77
  247.9 4.3 compare_select_fusion.16
  252.9 3.1 gather_fusion
  256.1 1.1 fusion.77
  259.8 4.3 compare_select_fusion.16
  264.8 3.1 gather_fusion
  268.0 1.1 fusion.77
  271.7 4.3 compare_select_fusion.16
  276.7 3.1 gather_fusion
  279.9 1.1 fusion.77
  283.6 4.3 compare_select_fusion.16
  288.6 3.1 gather_fusion
  291.8 1.1 fusion.77
  293.5 1.3 copy-done.6
  294.8 2.2 copy.49
  297.4 21.5 %broadcast_in_dim.154 = f32[1024,64,128]{2,1,0:T(8,128)} broadcast(f32[1024,64]{1,0:T(8,128)S(1)} %bitcast.151), dimensions={0,1} | broadcast | bytes 33816576 | tf_op jit(solution)/shard_map/broadcast_in_dim | solution.py:18
  318.8 42.5 %fusion.35 = bf16[512,8192]{1,0:T(8,128)(2,1)} fusion(bf16[512,1024]{0,1:T(8,128)(2,1)S(1)} %bitcast.147, f32[128,8,64,128]{3,2,1,0:T(8,128)} %bitcast.138, bf16[1024,8192]{1,0:T(8,128)(2,1)} %param.27), kind=kOutput, calls=%fused_computation.66 | convolution fusion | flops 8619294720 | bytes 59768832 | tf_op jit(solution)/shard_map/dot_general | solution.py:155
  362.2 103.0 %reduce-scatter.2.cloned.1.call-done = bf16[128,8192]{1,0:T(8,128)(2,1)} async-done(((bf16[512,8192]{1,0:T(8,128)(2,1)}), bf16[128,8192]{1,0:T(8,128)(2,1)}) %reduce-scatter.2.cloned.1.call-update) | async-done | bytes 2097168 | tf_op jit(solution)/shard_map/reduce_scatter | solution.py:154
  465.2 2.1 fusion.46
  467.3 1.3 copy-done.2
  469.4 39.3 %psum.7 = f32[4]{0:T(128)S(1)} all-reduce(f32[4]{0:T(128)S(1)} %select_reduce_fusion), channel_id=1, replica_groups=mesh['ctx'=8,'tp'=4] {'ctx','tp'}, use_global_device_ids=true, to_apply=%region_14.16 | all-reduce | flops 4 | bytes 32 | tf_op jit(solution)/shard_map/psum | solution.py:166
  (134 shorter events, 24.0 us)
Async XLA Ops:
  7.2 5.8 %copy-start.7 = (s32[8]{0:T(128)S(1)}, s32[8]{0:T(128)}, u32[]{:S(2)}) copy-start(s32[8]{0:T(128)} %param.31) | copy-start | bytes 100
  7.2 7.0 %copy-start = (s32[4096]{0:T(1024)S(1)}, s32[4096]{0:T(1024)}, u32[]{:S(2)}) copy-start(s32[4096]{0:T(1024)} %param.30) | copy-start | bytes 49156
  7.2 10.5 %copy-start.12 = (f32[64,2]{0,1:T(2,128)S(1)}, f32[64,2]{0,1:T(2,128)}, u32[]{:S(2)}) copy-start(f32[64,2]{0,1:T(2,128)} %param.24) | copy-start | bytes 1540
  7.2 10.6 %copy-start.13 = (f32[64,2]{0,1:T(2,128)S(1)}, f32[64,2]{0,1:T(2,128)}, u32[]{:S(2)}) copy-start(f32[64,2]{0,1:T(2,128)} %param.26) | copy-start | bytes 1540
  7.2 10.7 %copy-start.11 = (f32[64,8]{0,1:T(8,128)S(1)}, f32[64,8]{0,1:T(8,128)}, u32[]{:S(2)}) copy-start(f32[64,8]{0,1:T(8,128)} %param.22) | copy-start | bytes 6148
  7.2 96.1 %all-gather.4.cloned.1.call-start = ((), (), s32[]{:S(2)}) async-start(), calls=%async_computation.1 | async-start | bytes 10485760 | tf_op jit(solution)/shard_map/all_gather | solution.py:88
  12.9 146.2 %all-gather.6.cloned.1.call-start = ((), (), s32[]{:S(2)}) async-start(), calls=%async_computation.2 | async-start | bytes 2359296 | tf_op jit(solution)/shard_map/all_gather | solution.py:123
  17.5 24.7 %copy-start.14 = (s32[4]{0:T(128)}, s32[4]{0:T(128)S(1)}, u32[]{:S(2)}) copy-start(s32[4]{0:T(128)S(1)} %convert_reduce_fusion) | copy-start | bytes 52
  103.3 24.2 %copy-start.4 = (f32[512,64]{1,0:T(8,128)S(1)}, f32[512,64]{1,0:T(8,128)}, u32[]{:S(2)}) copy-start(f32[512,64]{1,0:T(8,128)} %get-tuple-element.362) | copy-start | bytes 393220
  123.2 1.6 copy-start.3
  125.6 9.4 %copy-start.5 = (f32[512,64]{1,0:T(8,128)S(1)}, f32[512,64]{1,0:T(8,128)}, u32[]{:S(2)}) copy-start(f32[512,64]{1,0:T(8,128)} %get-tuple-element.363) | copy-start | bytes 393220
  129.5 59.8 %all-gather.8.cloned.1.call-start = ((), (), s32[]{:S(2)}) async-start(), calls=%async_computation.3 | async-start | bytes 2359296 | tf_op jit(solution)/shard_map/all_gather | solution.py:124
  131.4 333.8 %reduce-scatter.2.cloned.1.call-start = ((), (), s32[]{:S(2)}) async-start(), calls=%async_computation.4 | async-start | bytes 10485760 | tf_op jit(solution)/shard_map/reduce_scatter | solution.py:154
  137.5 4.9 copy-start.8
  189.3 108.0 %copy-start.10 = (f32[8,64]{1,0:T(8,128)S(1)}, f32[8,64]{1,0:T(8,128)}, u32[]{:S(2)}) copy-start(f32[8,64]{1,0:T(8,128)} %param.28) | copy-start | bytes 6148
  293.5 1.3 copy-start.6
  361.4 0.7 copy-start.9
  361.4 103.8 %copy-start.1 = (bf16[128,8192]{1,0:T(8,128)(2,1)S(1)}, bf16[128,8192]{1,0:T(8,128)(2,1)}, u32[]{:S(2)}) copy-start(bf16[128,8192]{1,0:T(8,128)(2,1)} %param.19) | copy-start | bytes 6291460
  361.4 147.3 %copy-start.15 = (s32[4]{0:T(128)S(1)}, s32[4]{0:T(128)}, u32[]{:S(2)}) copy-start(s32[4]{0:T(128)} %copy-done.14) | copy-start | bytes 52
  467.3 1.3 copy-start.2
Sparse Core Ops, SparseCore 0:
  13.0 90.2 all-gather.3
  129.7 29.3 all-gather.5
  160.7 28.5 all-gather.7
  361.5 103.6 reduce-scatter.1
where the time goes:
time: 521 us; the launch traced here: 516 us
  waiting for transfers between devices  150 us (29%)
  local copies, waits for them, and re-layouts  128 us (25%)
  other arithmetic  97.4 us (19%)
  matrix products  75.5 us (14%)
  blocking collectives  39.3 us (8%)
  between operations  15.2 us (3%)
  loops' own time  10.9 us (2%)
    reduce_scatter x1, waiting for transfers between devices, on_device(): lax.psum_scatter(jnp.dot(attended, w_back, preferred_element_type=jnp.flo...  103 us
    broadcast_in_dim x8, local copies, waits for them, and re-layouts, dequant(): expanded = jnp.repeat(jnp.repeat(scales, BLOCK, 0), BLOCK, 1)  72.2 us
    dot_general x1, matrix products, on_device(): jnp.dot(attended, w_back, preferred_element_type=jnp.float32)  42.5 us
    psum x1, blocking collectives, on_device(): totals = lax.psum(partial_sums, ('ctx', 'tp'))  39.3 us
    gather x16, other arithmetic, one_block(): key_pos = jnp.take(span_of, source) * span_len + row_index % span_len  34.9 us
    all_gather x1, waiting for transfers between devices, on_device(): value_piece = lax.all_gather(values_here, 'ctx', axis=0, tiled=True)  30.2 us
    convert_element_type x2, other arithmetic, dequant(): return (stored.astype(jnp.float32) * expanded).astype(jnp.bfloat16)  27.1 us
    gather x8, local copies, waits for them, and re-layouts, one_block(): key_doc = jnp.take(doc_ids, key_pos)  25.1 us
  transfers between devices with their start and end apart: 4, of which 4 were waited for; matrix products, arithmetic and copies ran while one was open for 20% of the time, Pallas kernels for 0%

commit v1 on v0

v1 whole, which is shorter than its diff:
```python
import functools

import jax
import jax.numpy as jnp
from jax import lax
from jax.experimental import pallas as pl
from jax.experimental.pallas import tpu as pltpu
from jax.sharding import PartitionSpec as P

HDIM = 128
BLOCK = 128
NDOC = 4
F32 = jnp.float32
BF16 = jnp.bfloat16
ANY = pl.ANY
HBM = pltpu.HBM
VMEM = pltpu.VMEM
SMEM = pltpu.SMEM
MIB = 1 << 20


def params(mib):
    return pltpu.CompilerParams(vmem_limit_bytes=mib * MIB)


def cost(flops, moved):
    return pl.CostEstimate(flops=int(flops), bytes_accessed=int(moved), transcendentals=0)


def turn(values, cosine, sine):
    pieces = []
    for head in range(values.shape[1] // HDIM):
        one = values[:, head * HDIM : (head + 1) * HDIM]
        pieces.append(one * cosine + pltpu.roll(one, HDIM // 2, 1) * sine)
    return jnp.concatenate(pieces, 1)


def resident(value):
    return pltpu.with_memory_space_constraint(value, VMEM)


def outside(value):
    return pltpu.with_memory_space_constraint(value, HBM)


def normalize(parts, gain, normed):
    rows, half = parts[0].shape
    step, wide = 16, 1024
    for block in range(len(parts) // 2):
        pair = parts[2 * block : 2 * block + 2]

        @pl.loop(0, rows // step)
        def _(i):
            here = pl.ds(pl.multiple_of(i * step, step), step)
            there = pl.ds(pl.multiple_of(block * rows + i * step, step), step)
            square = jnp.zeros((step, wide), F32)
            for part in pair:
                for c in range(half // wide):
                    chunk = part[here, c * wide : (c + 1) * wide].astype(F32)
                    square = square + chunk * chunk
            factor = lax.rsqrt(jnp.sum(square, -1, keepdims=True) / (2 * half) + 1e-05)
            for side, part in enumerate(pair):
                for c in range(half // wide):
                    columns = slice(c * wide, (c + 1) * wide)
                    at = slice(side * half + c * wide, side * half + (c + 1) * wide)
                    chunk = part[here, columns].astype(F32)
                    normed[there, at] = (chunk * factor * gain[:, at]).astype(BF16)


def keys_and_values(normed, weight, cosine, sine, pair):
    key_cols = pair.shape[1] // 2
    product = jnp.dot(normed[...], weight[:, :key_cols], preferred_element_type=F32)
    pair[:, :key_cols] = turn(product, cosine[...], sine[...]).astype(BF16)
    product = jnp.dot(
        normed[...], weight[:, key_cols : 2 * key_cols], preferred_element_type=F32
    )
    pair[:, key_cols:] = product.astype(BF16)


def queries_of(normed, weight, skip, cosine, sine, query):
    tile = 2 * HDIM
    for start in range(0, query.shape[1], tile):
        product = jnp.dot(
            normed[...], weight[:, skip + start : skip + start + tile], preferred_element_type=F32
        )
        query[:, start : start + tile] = turn(product, cosine[...], sine[...]).astype(BF16)


def joint_body(count, *refs):
    stored, scales = refs[:count], refs[count : 2 * count]
    weight = refs[2 * count]
    slots, sems = refs[2 * count + 1 : 3 * count + 1], refs[3 * count + 1]
    depth = slots[0].shape[1]
    steps = weight.shape[0] // depth

    def fetch(i, slot):
        here = pl.ds(pl.multiple_of(i * depth, depth), depth)
        return [
            pltpu.make_async_copy(stored[n].at[here], slots[n].at[slot], sems.at[n, slot])
            for n in range(count)
        ]

    for copy in fetch(0, 0):
        copy.start()

    @pl.loop(0, steps)
    def _(i):
        slot = lax.rem(i, 2)

        @pl.when(i + 1 < steps)
        def _():
            for copy in fetch(i + 1, 1 - slot):
                copy.start()

        for copy in fetch(i, slot):
            copy.wait()
        for r in range(depth // BLOCK):
            out_rows = pl.ds(pl.multiple_of(i * depth + r * BLOCK, BLOCK), BLOCK)
            column = 0
            for n in range(count):
                for j in range(slots[n].shape[2] // BLOCK):
                    tile = slots[n][
                        slot, r * BLOCK : (r + 1) * BLOCK, j * BLOCK : (j + 1) * BLOCK
                    ].astype(F32)
                    factor = scales[n][i * (depth // BLOCK) + r, j]
                    weight[out_rows, column + j * BLOCK : column + (j + 1) * BLOCK] = (
                        tile * factor
                    ).astype(BF16)
                column += slots[n].shape[2]


def dequant_joint(stored, scales):
    width, depth = stored[0].shape[0], 512
    widths = [one.shape[1] for one in stored]
    return pl.pallas_call(
        functools.partial(joint_body, len(stored)),
        in_specs=[pl.BlockSpec(memory_space=HBM) for _ in widths]
        + [pl.BlockSpec(memory_space=SMEM) for _ in widths],
        out_specs=pl.BlockSpec(memory_space=VMEM),
        out_shape=VMEM((width, sum(widths)), BF16),
        scratch_shapes=[VMEM((2, depth, one), BF16) for one in widths]
        + [pltpu.SemaphoreType.DMA((len(widths), 2))],
        compiler_params=params(16),
        cost_estimate=cost(600 * width * sum(widths), 2 * width * sum(widths)),
    )(*[outside(one) for one in stored], *scales)


def keys_body(blocks, *refs):
    parts = refs[: 2 * blocks]
    gain, weight, cosine, sine, normed, pair = refs[2 * blocks :]
    normalize(parts, gain, normed)
    keys_and_values(normed, weight, cosine, sine, pair)


def project_keys(parts, rows, gain, weight, key_cols, cosine, sine):
    blocks = len(parts) // 2
    width = weight.shape[0]
    half, total = width // 2, rows * blocks
    inside = pl.BlockSpec(memory_space=VMEM)
    return pl.pallas_call(
        functools.partial(keys_body, blocks),
        grid=(1,),
        in_specs=[pl.BlockSpec((rows, half), lambda k, at=at: (0, at)) for _, at in parts]
        + [pl.BlockSpec((1, width), lambda k: (0, 0)), inside, inside, inside],
        out_specs=[pl.BlockSpec((total, width), lambda k: (0, 0)), inside],
        out_shape=[
            jax.ShapeDtypeStruct((total, width), BF16),
            jax.ShapeDtypeStruct((total, 2 * key_cols), BF16),
        ],
        compiler_params=params(16),
        cost_estimate=cost(8 * total * width * key_cols, 6 * total * width),
    )(*[one for one, _ in parts], gain, resident(weight), cosine, sine)


def queries_body(skip, normed, weight, cosine, sine, query):
    queries_of(normed, weight, skip, cosine, sine, query)


def project_queries(normed, weight, skip, cosine, sine):
    total, width = normed.shape
    columns = weight.shape[1] - skip
    inside = pl.BlockSpec(memory_space=VMEM)
    return pl.pallas_call(
        functools.partial(queries_body, skip),
        in_specs=[inside] * 4,
        out_specs=inside,
        out_shape=jax.ShapeDtypeStruct((total, columns), BF16),
        compiler_params=params(16),
        cost_estimate=cost(4 * total * width * columns, 4 * total * width),
    )(normed, resident(weight), cosine, sine)


def back_body(stored, scales, out, slots, sems):
    depth, width = slots.shape[1:]
    steps = stored.shape[0] // depth

    def fetch(i, slot):
        here = pl.ds(pl.multiple_of(i * depth, depth), depth)
        return pltpu.make_async_copy(stored.at[here], slots.at[slot], sems.at[slot])

    fetch(0, 0).start()

    @pl.loop(0, steps)
    def _(i):
        slot = lax.rem(i, 2)

        @pl.when(i + 1 < steps)
        def _():
            fetch(i + 1, 1 - slot).start()

        fetch(i, slot).wait()
        here = pl.ds(pl.multiple_of(i * depth, depth), depth)
        for j in range(width // BLOCK):
            there = slice(j * BLOCK, (j + 1) * BLOCK)
            factor = scales[i * depth // BLOCK, j]
            out[here, there] = (slots[slot, :, there].astype(F32) * factor).astype(BF16)


def dequant_back(stored, scales):
    rows, width = stored.shape
    depth = BLOCK
    return pl.pallas_call(
        back_body,
        in_specs=[pl.BlockSpec(memory_space=HBM), pl.BlockSpec(memory_space=SMEM)],
        out_specs=pl.BlockSpec(memory_space=VMEM),
        out_shape=VMEM((rows, width), BF16),
        scratch_shapes=[VMEM((2, depth, width), BF16), pltpu.SemaphoreType.DMA((2,))],
        compiler_params=params(8),
        cost_estimate=cost(8 * rows * width, 2 * rows * width),
    )(outside(stored), scales)


def toward_body(weight, vector, toward):
    rows, width = weight.shape
    step = 32

    @pl.loop(0, rows // step)
    def _(i):
        here = pl.ds(pl.multiple_of(i * step, step), step)
        run = jnp.zeros((step, BLOCK), F32)
        for j in range(width // BLOCK):
            there = slice(j * BLOCK, (j + 1) * BLOCK)
            run = run + weight[here, there].astype(F32) * vector[:, there]
        toward[here, :] = jnp.broadcast_to(jnp.sum(run, 1, keepdims=True), (step, BLOCK))


def toward_score(weight, vector):
    rows, width = weight.shape
    inside = pl.BlockSpec(memory_space=VMEM)
    return pl.pallas_call(
        toward_body,
        in_specs=[inside] * 2,
        out_specs=inside,
        out_shape=jax.ShapeDtypeStruct((rows, BLOCK), F32),
        compiler_params=params(8),
        cost_estimate=cost(8 * rows * width, 2 * rows * width),
    )(resident(weight), vector)


def halves_body(one, two, low, high):
    low[...] = one[...]
    high[...] = two[...]


def halves(one, two):
    rows, width = one.shape
    steps = 4
    tile = width // 2 // steps
    first = pl.BlockSpec((rows, tile), lambda j: (0, j))
    second = pl.BlockSpec((rows, tile), lambda j: (0, steps + j))
    return pl.pallas_call(
        halves_body,
        grid=(steps,),
        in_specs=[first, second],
        out_specs=[first, first],
        out_shape=[jax.ShapeDtypeStruct((rows, width // 2), BF16)] * 2,
        compiler_params=params(8),
        cost_estimate=cost(0, 4 * rows * width),
    )(one, two)


def attend_body(sizes, *refs):
    units, rows, kv_heads, group, chunk, kinds = sizes
    meta = refs[0]
    many = len(kinds)
    queries = refs[1 : 1 + many]
    held = refs[1 + many : 1 + many + many * units]
    out, pool, asked, kv_sem, q_sem = refs[1 + many + many * units :]
    length = sum(len(flips) for flips in kinds) * rows
    key_cols = kv_heads * HDIM
    mine = meta[0]
    starts = [meta[1 + d] for d in range(NDOC)]
    member = meta[1 + NDOC]
    span_at = 2 + NDOC

    def doc_start(position):
        found = jnp.int32(0)
        for one in starts:
            found = jnp.where(one <= position, one, found)
        return found

    first_span = doc_start(mine * length) // length
    q_copies = [
        pltpu.make_async_copy(
            queries[i],
            asked.at[pl.ds(flips[0] * rows, len(flips) * rows)],
            q_sem.at[i],
        )
        for i, flips in enumerate(kinds)
    ]
    for copy in q_copies:
        copy.start()

    def copies(unit, go):
        span = meta[span_at + unit]

        @pl.when((span >= first_span) & (span <= mine))
        def _():
            count = 0
            for kind, flips in enumerate(kinds):
                source = held[kind * units + unit]
                for piece, flip in enumerate(flips):
                    place = pl.multiple_of(
                        span * length + (member ^ flip) * rows, BLOCK
                    )
                    copy = pltpu.make_async_copy(
                        source.at[pl.ds(piece * rows, rows)],
                        pool.at[pl.ds(place, rows)],
                        kv_sem.at[unit, count],
                    )
                    count += 1
                    if go:
                        copy.start()
                    else:
                        copy.wait()

    for unit in range(units):
        copies(unit, True)
    for copy in q_copies:
        copy.wait()
    for unit in range(units):
        copies(unit, False)

    factor = HDIM ** (-0.5) * 1.4426950408889634

    @pl.loop(0, length // BLOCK)
    def _(index):
        at = pl.multiple_of(index * BLOCK, BLOCK)
        flip = at // rows
        position = mine * length + (member ^ flip) * rows + at % rows
        low = doc_start(position) // chunk
        high = (position + BLOCK - 1) // chunk
        row_pos = position + lax.broadcasted_iota(jnp.int32, (BLOCK, chunk), 0)
        row_start = doc_start(row_pos)
        lane = lax.broadcasted_iota(jnp.int32, (BLOCK, chunk), 1)
        for head in range(kv_heads):
            query = jnp.concatenate(
                [
                    asked[
                        pl.ds(at, BLOCK),
                        (head * group + g) * HDIM : (head * group + g + 1) * HDIM,
                    ]
                    for g in range(group)
                ],
                0,
            )

            def one_chunk(c, state):
                peak, total, acc = state
                here = pl.ds(pl.multiple_of(c * chunk, chunk), chunk)
                key = pool[here, head * HDIM : (head + 1) * HDIM]
                value = pool[here, key_cols + head * HDIM : key_cols + (head + 1) * HDIM]
                scores = lax.dot_general(
                    query, key, (((1,), (1,)), ((), ())), preferred_element_type=F32
                )
                key_pos = lane + c * chunk
                seen = (key_pos <= row_pos) & (key_pos >= row_start)
                scores = jnp.where(
                    seen[None], scores.reshape(group, BLOCK, chunk) * factor, -1e30
                ).reshape(group * BLOCK, chunk)
                higher = jnp.maximum(peak, jnp.max(scores, -1, keepdims=True))
                weights = jnp.exp2(scores - higher)
                fading = jnp.exp2(peak - higher)
                total = total * fading + jnp.sum(weights, -1, keepdims=True)
                acc = acc * fading + jnp.dot(
                    weights.astype(BF16), value, preferred_element_type=F32
                )
                return higher, total, acc

            state = (
                jnp.full((group * BLOCK, 1), -1e30, F32),
                jnp.zeros((group * BLOCK, 1), F32),
                jnp.zeros((group * BLOCK, HDIM), F32),
            )
            peak, total, acc = lax.fori_loop(low, high + 1, one_chunk, state)
            result = (acc / total).astype(BF16)
            for g in range(group):
                out[
                    pl.ds(at, BLOCK), (head * group + g) * HDIM : (head * group + g + 1) * HDIM
                ] = result[g * BLOCK : (g + 1) * BLOCK]


def attend(meta, queries, held, units, rows, kv_heads, group, kinds):
    blocks = sum(len(flips) for flips in kinds)
    length = blocks * rows
    columns = kv_heads * group * HDIM
    chunk = 2 * BLOCK
    sizes = (units, rows, kv_heads, group, chunk, kinds)
    return pl.pallas_call(
        functools.partial(attend_body, sizes),
        in_specs=[pl.BlockSpec(memory_space=SMEM)]
        + [pl.BlockSpec(memory_space=ANY)] * (len(kinds) * (1 + units)),
        out_specs=pl.BlockSpec(memory_space=VMEM),
        out_shape=jax.ShapeDtypeStruct((length, columns), BF16),
        scratch_shapes=[
            VMEM((units * length, 2 * kv_heads * HDIM), BF16),
            VMEM((length, columns), BF16),
            pltpu.SemaphoreType.DMA((units, blocks)),
            pltpu.SemaphoreType.DMA((len(kinds),)),
        ],
        compiler_params=params(20),
        cost_estimate=cost(8 * length * columns * 1024, 8 * MIB),
    )(meta, *queries, *held)


def term_of(rows_of, weight, start, width):
    return jnp.dot(
        rows_of, weight[:, start : start + width], preferred_element_type=F32
    ).astype(BF16)


def outward_body(starts, attended, weight, xo, yo):
    rows = attended.shape[0] // 4
    tile = 512
    for start in range(0, xo.shape[1], tile):
        here = slice(start, start + tile)
        for block, place in ((1, 0), (3, rows)):
            xo[place : place + rows, here] = term_of(
                attended[block * rows : (block + 1) * rows, :], weight, starts[0] + start, tile
            )
        for block, place in ((2, 0), (3, rows)):
            yo[place : place + rows, here] = term_of(
                attended[block * rows : (block + 1) * rows, :], weight, starts[1] + start, tile
            )


def outward(attended, weight, start, span):
    depth, width = weight.shape
    rows = attended.shape[0] // 4
    inside = pl.BlockSpec(memory_space=VMEM)
    return pl.pallas_call(
        functools.partial(outward_body, (start, width // 2 + start)),
        in_specs=[inside] * 2,
        out_specs=[inside] * 2,
        out_shape=[jax.ShapeDtypeStruct((2 * rows, span), BF16)] * 2,
        compiler_params=params(12),
        cost_estimate=cost(16 * rows * depth * span, 8 * rows * span),
    )(attended, resident(weight))


def kept_body(attended, weight, inner, term):
    rows = attended.shape[0] // 4
    width = weight.shape[1]
    tile = 512
    for start in range(0, width, tile):
        here = slice(start, start + tile)
        block = 2 if start < width // 2 else 1
        inner[:, here] = term_of(
            attended[block * rows : (block + 1) * rows, :], weight, start, tile
        )
        term[:, here] = term_of(attended[:rows, :], weight, start, tile)


def kept_terms(attended, weight):
    depth, width = weight.shape
    rows = attended.shape[0] // 4
    inside = pl.BlockSpec(memory_space=VMEM)
    return pl.pallas_call(
        kept_body,
        in_specs=[inside] * 2,
        out_specs=[inside] * 2,
        out_shape=[jax.ShapeDtypeStruct((rows, width), BF16)] * 2,
        compiler_params=params(12),
        cost_estimate=cost(8 * rows * depth * width, 4 * rows * width),
    )(attended, resident(weight))


def block_body(block, blocks, attended, weight, out):
    rows = attended.shape[0] // blocks
    for start in range(0, weight.shape[1], 512):
        out[:, start : start + 512] = term_of(
            attended[block * rows : (block + 1) * rows, :], weight, start, 512
        )


def block_term(attended, weight, block, blocks):
    depth, width = weight.shape
    rows = attended.shape[0] // blocks
    inside = pl.BlockSpec(memory_space=VMEM)
    return pl.pallas_call(
        functools.partial(block_body, block, blocks),
        in_specs=[inside] * 2,
        out_specs=inside,
        out_shape=jax.ShapeDtypeStruct((rows, width), BF16),
        compiler_params=params(12),
        cost_estimate=cost(2 * rows * depth * width, 2 * rows * width),
    )(attended, resident(weight))


def finish_body(token, term, near_x, near_y, far_y, far_x, *rest):
    out = rest[-1]

    def add(near, far):
        mixed = term[...].astype(F32) + near[...].astype(F32) + far[...].astype(F32)
        out[...] = (token[...].astype(F32) + mixed).astype(BF16)

    @pl.when(pl.program_id(0) == 0)
    def _():
        add(near_x, far_y)

    @pl.when(pl.program_id(0) == 1)
    def _():
        add(near_y, far_x)


def finish(token, term, near_x, near_y, far_y, far_x, before, part, parts):
    rows, width = token.shape
    span = width // 2 // parts
    tile = min(span, 1024)
    steps = span // tile
    half = width // 2 // tile

    def whole(h, j):
        return (0, h * half + part * steps + j)

    low = pl.BlockSpec((rows, tile), lambda h, j: (0, jnp.where(h == 0, j, steps - 1)))
    high = pl.BlockSpec((rows, tile), lambda h, j: (0, jnp.where(h == 0, 0, j)))
    specs = [pl.BlockSpec((rows, tile), whole)] * 2 + [low, high, low, high]
    operands = [token, term, near_x, near_y, far_y, far_x]
    aliases = {}
    if before is not None:
        specs.append(pl.BlockSpec(memory_space=ANY))
        operands.append(before)
        aliases = {6: 0}
    return pl.pallas_call(
        finish_body,
        grid=(2, steps),
        in_specs=specs,
        out_specs=pl.BlockSpec((rows, tile), whole),
        out_shape=jax.ShapeDtypeStruct((rows, width), BF16),
        input_output_aliases=aliases,
        compiler_params=params(40),
        cost_estimate=cost(rows * span, 20 * rows * span),
    )(*operands)


def on_device(
    tokens,
    norm_gain,
    w_query,
    query_scale,
    w_key,
    key_scale,
    w_value,
    value_scale,
    w_out,
    out_scale,
    score_vec,
    doc_ids,
    span_of,
):
    rows, width = tokens.shape
    half = width // 2
    n_ctx = lax.axis_size("ctx")
    n_tp = lax.axis_size("tp")
    length = n_tp * rows
    slot = lax.axis_index("ctx")
    member = lax.axis_index("tp")
    span_pos = span_of[slot]

    def flip_tp(value, flip):
        return lax.ppermute(value, "tp", [(i, i ^ flip) for i in range(n_tp)])

    query_cols, key_cols = w_query.shape[1], w_key.shape[1]
    kv_heads = key_cols // HDIM
    group = query_cols // key_cols
    gain = norm_gain[None, :]

    doc_iota = jnp.arange(NDOC, dtype=jnp.int32)
    counts = jnp.sum((doc_ids[None, :] == doc_iota[:, None]).astype(jnp.int32), 1)
    starts = jnp.sum(jnp.where(doc_iota[None, :] < doc_iota[:, None], counts[None, :], 0), 1)
    row_iota = jnp.arange(length, dtype=jnp.int32)
    position = span_pos * length + (member ^ (row_iota // rows)) * rows + row_iota % rows
    begun = starts[None, :] <= position[:, None]
    document = jnp.sum(begun.astype(jnp.int32), 1) - 1
    relative = position - jnp.max(jnp.where(begun, starts[None, :], 0), 1)
    frequency = 500000.0 ** (-2.0 * jnp.arange(HDIM // 2).astype(F32) / HDIM)
    angles = relative.astype(F32)[:, None] * frequency[None, :]
    cosine, sine = jnp.cos(angles), jnp.sin(angles)
    cosine = jnp.concatenate([cosine, cosine], 1)
    sine = jnp.concatenate([-sine, sine], 1)

    def exchange_along(value):
        return [value] + [
            lax.ppermute(value, "ctx", [(i, (i + 2 * step) % n_ctx) for i in range(n_ctx)])
            for step in range(1, n_ctx // 2)
        ]

    def exchange_across(held):
        return held + [
            lax.ppermute(one, "ctx", [(i, i ^ 1) for i in range(n_ctx)]) for one in held
        ]

    sources = [(slot - 2 * step) % n_ctx for step in range(n_ctx // 2)]
    sources += [((slot ^ 1) - 2 * step) % n_ctx for step in range(n_ctx // 2)]
    meta = jnp.concatenate(
        [
            span_pos[None],
            starts,
            member[None].astype(jnp.int32),
            jnp.take(span_of, jnp.stack(sources)),
        ]
    ).astype(jnp.int32)

    square = n_tp == 4
    if square:
        kinds = ((0,), (1, 2), (3,))
    else:
        kinds = ((0,),) + tuple((i, i + 1) for i in range(1, n_tp - 1, 2)) + ((n_tp - 1,),)
    tables = [
        tuple(
            one[flips[0] * rows : (flips[-1] + 1) * rows] for one in (cosine, sine)
        )
        for flips in kinds
    ]
    token_score = jnp.dot(tokens, score_vec, preferred_element_type=F32)
    vector = score_vec.astype(F32)[None, :]
    gain, tables, token_score, vector, meta, document, counts = lax.optimization_barrier(
        (gain, tables, token_score, vector, meta, document, counts)
    )
    near = {flip: flip_tp(tokens, flip) for flip in ((1, 2) if square else range(1, n_tp))}

    weight = dequant_joint((w_key, w_value, w_query), (key_scale, value_scale, query_scale))
    normed, own_pair = project_keys(
        [(tokens, 0), (tokens, 1)], rows, gain, weight, key_cols, *tables[0]
    )
    held = exchange_across(exchange_along(own_pair))
    own_query = project_queries(normed, weight, 2 * key_cols, *tables[0])

    if square:
        near[1], near[2], own_query = lax.optimization_barrier((near[1], near[2], own_query))
        low, high = halves(near[1], near[2])
        far_low, far_high = flip_tp(low, 2), flip_tp(high, 1)
    queries = [own_query]
    for flips, table in zip(kinds[1:], tables[1:]):
        if square and flips == (3,):
            far_low, far_high, queries = lax.optimization_barrier((far_low, far_high, queries))
            parts = [(far_low, 0), (far_high, 0)]
        else:
            parts = [(near[flip], side) for flip in flips for side in range(2)]
        normed, pair = project_keys(parts, rows, gain, weight, key_cols, *table)
        along = exchange_along(pair)
        query = project_queries(normed, weight, 2 * key_cols, *table)
        if flips == kinds[-1]:
            query, late_scale = lax.optimization_barrier((query, out_scale))
            back = dequant_back(w_out, late_scale)
            along, query, back = lax.optimization_barrier((along, query, back))
        held += exchange_across(along)
        queries.append(query)

    attended = attend(meta, queries, held, n_ctx, rows, kv_heads, group, kinds)

    def all_sum(value, axis, size, step):
        while step < size:
            value = value + lax.ppermute(value, axis, [(i, i ^ step) for i in range(size)])
            step *= 2
        return value

    def span_sums(attended, toward):
        row_score = jnp.sum(attended.astype(F32) * toward[:, 0][None, :], 1)
        row_score = row_score + jnp.concatenate([token_score, jnp.zeros((length - rows,), F32)])
        own = document[:, None] == doc_iota[None, :]
        partial = jnp.sum(jnp.where(own, row_score[:, None], 0.0), 0)
        return all_sum(partial, "ctx", n_ctx, 1)

    if not square:
        partial = span_sums(attended, toward_score(back, vector))
        mixed = block_term(attended, back, 0, n_tp).astype(F32)
        for flip in range(1, n_tp):
            mixed = mixed + flip_tp(block_term(attended, back, flip, n_tp), flip).astype(F32)
        totals = all_sum(partial, "tp", n_tp, 1)
        return ((tokens.astype(F32) + mixed).astype(BF16), totals / counts.astype(F32))

    parts = 2
    span = half // parts
    sent = []
    for part in range(parts):
        out_x, out_y = outward(attended, back, part * span, span)
        sent.append((flip_tp(out_x, 1), flip_tp(out_y, 2)))
        attended, out_x, out_y = lax.optimization_barrier((attended, out_x, out_y))
    inner, term = kept_terms(attended, back)
    partial = span_sums(attended, toward_score(back, vector))

    def onward(got, start):
        ours = inner[:, start : start + span].astype(F32)
        return (ours + got[rows:].astype(F32)).astype(BF16)

    hidden = None
    for part in range(parts):
        near_x, near_y = sent[part]
        near_x, near_y, inner, term, partial = lax.optimization_barrier(
            (near_x, near_y, inner, term, partial)
        )
        on_y, on_x = onward(near_x, part * span), onward(near_y, half + part * span)
        far_y, far_x = flip_tp(on_y, 2), flip_tp(on_x, 1)
        if part < 2:
            partial, on_y, on_x = lax.optimization_barrier((partial, on_y, on_x))
            partial = partial + flip_tp(partial, 1 + part)
        hidden = finish(tokens, term, near_x, near_y, far_y, far_x, hidden, part, parts)
    return (hidden, partial / counts.astype(F32))


def solution(mesh):
    return jax.shard_map(
        on_device,
        mesh=mesh,
        in_specs=(
            P(("ctx", "tp"), None),
            P(),
            P(None, "tp"),
            P(None, "tp"),
            P(None, "tp"),
            P(None, "tp"),
            P(None, "tp"),
            P(None, "tp"),
            P("tp", None),
            P("tp", None),
            P(),
            P(),
            P(),
        ),
        out_specs=(P(("ctx", "tp"), None), P()),
        check_vma=False,
    )
```

time: 521 us -> 235 us (0.45)
  local copies, waits for them, and re-layouts: 128 us -> 20.4 us
  Pallas kernels: 0 us -> 92.8 us
  other arithmetic: 97.4 us -> 5.58 us
  matrix products: 75.5 us -> 0.64 us
  waiting for transfers between devices: 150 us -> 77.1 us
  blocking collectives: 39.3 us -> 0 us
  starting transfers between devices: 0.16 us -> 35.1 us
  between operations: 15.2 us -> 1.55 us
  loops' own time: 10.9 us -> 0 us
    reduce_scatter x1 -> x0, waiting for transfers between devices: 103 us -> none  [on_device(): lax.psum_scatter(jnp.dot(attended, w_back, preferred_element_type=jnp.flo...]
    pallas_call x0 -> x16, Pallas kernels: none -> 92.8 us  [the longest x1 19.5 us: attend(): pl.pallas_call(functools.partial(attend_body, sizes), in_specs=[pl.BlockS...]
    ppermute x0 -> x38, waiting for transfers between devices: none -> 77.1 us  [the longest x14 49.3 us: flip_tp(): return lax.ppermute(value, 'tp', [(i, i ^ flip) for i in range(n_tp)])]
    dot_general x7 -> x1, matrix products: 75.5 us -> 0.64 us  [on_device(): token_score = jnp.dot(tokens, score_vec, preferred_element_type=F32)]
    broadcast_in_dim x8 -> x0, local copies, waits for them, and re-layouts: 72.2 us -> none  [dequant(): expanded = jnp.repeat(jnp.repeat(scales, BLOCK, 0), BLOCK, 1)]
    all_gather x3 -> x0, waiting for transfers between devices: 46.4 us -> none  [the longest x1 30.2 us: on_device(): value_piece = lax.all_gather(values_here, 'ctx', axis=0, tiled=True)]
    psum x1 -> x0, blocking collectives: 39.3 us -> none  [on_device(): totals = lax.psum(partial_sums, ('ctx', 'tp'))]
    ppermute x0 -> x38, starting transfers between devices: none -> 35.1 us  [the longest x14 16 us: flip_tp(): return lax.ppermute(value, 'tp', [(i, i ^ flip) for i in range(n_tp)])]
  transfers between devices with their start and end apart: 4 -> 38, of which waited for: 4 -> 14; matrix products, arithmetic and copies ran while one was open for 20% -> 4% of each run, Pallas kernels for 0% -> 29%
where the time goes in v1:
time: 235 us; the launch traced here: 233 us
  Pallas kernels  92.8 us (39%)
  waiting for transfers between devices  77.1 us (33%)
  starting transfers between devices  35.1 us (15%)
  local copies, waits for them, and re-layouts  20.4 us (9%)
  other arithmetic  5.58 us (2%)
    ppermute x14, waiting for transfers between devices, flip_tp(): return lax.ppermute(value, 'tp', [(i, i ^ flip) for i in range(n_tp)])  49.3 us
    pallas_call x1, Pallas kernels, attend(): pl.pallas_call(functools.partial(attend_body, sizes), in_specs=[pl.BlockS...  19.5 us
    ppermute x9, waiting for transfers between devices, exchange_along(): lax.ppermute(value, 'ctx', [(i, (i + 2 * step) % n_ctx) for i in range(n_...  19 us
    unnamed x20, local copies, waits for them, and re-layouts  17.5 us
    pallas_call x1, Pallas kernels, dequant_joint(): pl.pallas_call(functools.partial(joint_body, len(stored)), in_specs=[pl.B...  17.1 us
    ppermute x14, starting transfers between devices, flip_tp(): return lax.ppermute(value, 'tp', [(i, i ^ flip) for i in range(n_tp)])  16 us
    ppermute x9, starting transfers between devices, exchange_along(): lax.ppermute(value, 'ctx', [(i, (i + 2 * step) % n_ctx) for i in range(n_...  13.4 us
    pallas_call x3, Pallas kernels, project_keys(): pl.pallas_call(functools.partial(keys_body, blocks), grid=(1,), in_specs=...  13.1 us
  transfers between devices with their start and end apart: 38, of which 14 were waited for; matrix products, arithmetic and copies ran while one was open for 4% of the time, Pallas kernels for 29%

profile of v1, /device:TPU:0, one launch (start us, length us, event | category | flops | bytes accessed | tf_op | source)
XLA Modules:
  0.0 233.2 jit_solution(11022531405201869879)
XLA Ops:
  0.6 3.0 %collective-permute-start = (bf16[128,8192]{1,0:T(8,128)(2,1)}, bf16[128,8192]{1,0:T(8,128)(2,1)}, u32[]{:S(2)}, u32[]{:S(2)}) collective-permute-start(bf16[128,8192]{1,0:T(8,128)(2,1)} %token_.3), channel_id=1, source_target_pairs={{0,1},{1,0},{2,3},{3,2},{4,5},{5,4},{6,7},{7,6},{8,9},{9,8},{10,11... | collective-permute-start | bytes 6291464 | tf_op jit(solution)/shard_map/ppermute | solution.py:582
  3.6 1.5 collective-permute-start.1
  5.2 0.7 reshape.406
  5.9 0.7 broadcast_in_dim.71
  6.8 1.3 gather_fusion
  8.1 1.2 dynamic_slice.3
  9.3 0.9 convert_reduce_fusion
  11.0 1.0 fusion.2
  12.0 0.6 pad_add_fusion.1.refs_0_
  13.1 0.6 convolution_bitcast_fusion
  14.0 17.1 %shard_map.140.refs_3_.weight.refs_5_ = bf16[8192,1536]{1,0:T(8,128)(2,1)S(1)} custom-call(bf16[8192,256]{1,0:T(8,128)(2,1)} %refs_0_.2, bf16[8192,256]{1,0:T(8,128)(2,1)} %refs_1_.2, bf16[8192,1024]{1,0:T(8,128)(2,1)} %refs_2_.1, f32[64,2]{1,0:T(8,128)S(1)} %copy.22.refs_3_, f32[64,2]{1,0:T(8,128)S(1)} %copy.23.refs_4_, f32[64,8]{1,0:T(8,128)S(1)} %copy.24.refs_5_), custom_call_target="tpu_custom_call" | custom-call | flops 7549747200 | bytes 25165824 | tf_op jit(solution)/shard_map/pallas_call | solution.py:135
  31.2 8.3 %copy-done = bf16[8192,1536]{1,0:T(8,128)(2,1)} copy-done((bf16[8192,1536]{1,0:T(8,128)(2,1)}, bf16[8192,1536]{1,0:T(8,128)(2,1)S(1)}, u32[]{:S(2)}) %copy-start) | copy-done | bytes 25165848
  39.5 8.2 %copy-done.1 = bf16[8192,1536]{1,0:T(8,128)(2,1)S(1)} copy-done((bf16[8192,1536]{1,0:T(8,128)(2,1)S(1)}, bf16[8192,1536]{1,0:T(8,128)(2,1)}, u32[]{:S(2)}) %copy-start.1) | copy-done | bytes 25165848
  47.6 2.9 %shard_map.141 = (bf16[128,8192]{1,0:T(8,128)(2,1)S(1)}, bf16[128,512]{1,0:T(8,128)(2,1)S(1)}) custom-call(bf16[128,8192]{1,0:T(8,128)(2,1)S(1)} %copy-done.2, bf16[128,8192]{1,0:T(8,128)(2,1)S(1)} %copy-done.2, f32[1,8192]{1,0:T(1,128)S(1)} %bitcast.26, bf16[8192,1536]{1,0:T(8,128)(2,1)S(1)} %copy-done.1, f32[128,128]{1,0:T(8,128)S(1)} %get-tuple-element.59.refs_4_.cosine, ...), custom_call_target="tpu_custom_call" | custom-call | flops 2147483648 | bytes 6291456 | tf_op jit(solution)/shard_map/pallas_call | solution.py:160
  50.5 1.6 collective-permute-start.7
  52.1 2.6 %collective-permute-start.8 = (bf16[128,512]{1,0:T(8,128)(2,1)S(1)}, bf16[128,512]{1,0:T(8,128)(2,1)S(1)}, u32[]{:S(2)}, u32[]{:S(2)}) collective-permute-start(bf16[128,512]{1,0:T(8,128)(2,1)S(1)} %get-tuple-element.81.refs_4_), channel_id=1, source_target_pairs={{0,16},{4,20},{8,24},{12,28},{16,0},{20,4},{24,8},{28,12},{1,17},{... | collective-permute-start | bytes 393224 | tf_op jit(solution)/shard_map/ppermute | solution.py:605
  54.7 1.4 collective-permute-start.9
  56.1 2.4 %shard_map.142.refs_1_ = bf16[128,1024]{1,0:T(8,128)(2,1)S(1)} custom-call(bf16[128,8192]{1,0:T(8,128)(2,1)S(1)} %get-tuple-element.61.normed, bf16[8192,1536]{1,0:T(8,128)(2,1)S(1)} %copy-done.1, f32[128,128]{1,0:T(8,128)S(1)} %get-tuple-element.59.refs_4_.cosine, f32[128,128]{1,0:T(8,128)S(1)} %get-tuple-element.60.refs_5_.sine), custom_call_target="tpu_custom_call" | custom-call | flops 4294967296 | bytes 4194304 | tf_op jit(solution)/shard_map/pallas_call | solution.py:183
  58.5 2.4 %shard_map.143 = (bf16[128,4096]{1,0:T(8,128)(2,1)S(1)}, bf16[128,4096]{1,0:T(8,128)(2,1)S(1)}) custom-call(bf16[128,8192]{1,0:T(8,128)(2,1)} %collective-permute-done.one.refs_0_.refs_1_, bf16[128,8192]{1,0:T(8,128)(2,1)} %collective-permute-done.1.two.refs_2_.refs_3_), custom_call_target="tpu_custom_call" | custom-call | bytes 4194304 | tf_op jit(solution)/shard_map/pallas_call | solution.py:271
  61.0 0.6 collective-permute-start.2
  61.6 0.5 collective-permute-start.3
  62.1 7.4 %shard_map.144 = (bf16[256,8192]{1,0:T(8,128)(2,1)S(1)}, bf16[256,512]{1,0:T(8,128)(2,1)S(1)}) custom-call(bf16[128,8192]{1,0:T(8,128)(2,1)} %collective-permute-done.one.refs_0_.refs_1_, bf16[128,8192]{1,0:T(8,128)(2,1)} %collective-permute-done.one.refs_0_.refs_1_, bf16[128,8192]{1,0:T(8,128)(2,1)} %collective-permute-done.1.two.refs_2_.refs_3_, ...), custom_call_target="tpu_custom_call" | custom-call | flops 4294967296 | bytes 12582912 | tf_op jit(solution)/shard_map/pallas_call | solution.py:160
  69.6 0.9 collective-permute-start.14
  70.5 4.6 %shard_map.145.refs_2_ = bf16[256,1024]{1,0:T(8,128)(2,1)S(1)} custom-call(bf16[256,8192]{1,0:T(8,128)(2,1)S(1)} %get-tuple-element.69.normed, bf16[8192,1536]{1,0:T(8,128)(2,1)S(1)} %copy-done.1, f32[256,128]{1,0:T(8,128)S(1)} %fusion.1.refs_6_.cosine, f32[256,128]{1,0:T(8,128)S(1)} %fusion.refs_7_.sine), custom_call_target="tpu_custom_call" | custom-call | flops 8589934592 | bytes 8388608 | tf_op jit(solution)/shard_map/pallas_call | solution.py:183
  75.2 9.4 %collective-permute-done.2.refs_0_ = bf16[128,4096]{1,0:T(8,128)(2,1)S(1)} collective-permute-done((bf16[128,4096]{1,0:T(8,128)(2,1)S(1)}, bf16[128,4096]{1,0:T(8,128)(2,1)S(1)}, u32[]{:S(2)}, u32[]{:S(2)}) %collective-permute-start.2) | collective-permute-done | bytes 1048608 | tf_op jit(solution)/shard_map/ppermute | solution.py:582
  85.1 0.5 collective-permute-start.15
  85.6 2.6 %collective-permute-start.16 = (bf16[256,512]{1,0:T(8,128)(2,1)S(1)}, bf16[256,512]{1,0:T(8,128)(2,1)S(1)}, u32[]{:S(2)}, u32[]{:S(2)}) collective-permute-start(bf16[256,512]{1,0:T(8,128)(2,1)S(1)} %get-tuple-element.82.refs_12_), channel_id=1, source_target_pairs={{0,24},{4,28},{8,0},{12,4},{16,8},{20,12},{24,16},{28,20},{1,25},{... | collective-permute-start | bytes 786440 | tf_op jit(solution)/shard_map/ppermute | solution.py:605
  88.1 2.8 %shard_map.146 = (bf16[128,8192]{1,0:T(8,128)(2,1)S(1)}, bf16[128,512]{1,0:T(8,128)(2,1)S(1)}) custom-call(bf16[128,4096]{1,0:T(8,128)(2,1)S(1)} %collective-permute-done.2.refs_0_, bf16[128,4096]{1,0:T(8,128)(2,1)S(1)} %collective-permute-done.3.refs_1_, f32[1,8192]{1,0:T(1,128)S(1)} %bitcast.28, bf16[8192,1536]{1,0:T(8,128)(2,1)S(1)} %copy-done.1, ...), custom_call_target="tpu_custom_call" | custom-call | flops 2147483648 | bytes 6291456 | tf_op jit(solution)/shard_map/pallas_call | solution.py:160
  91.0 1.9 collective-permute-start.5
  92.9 2.0 collective-permute-start.6
  94.8 6.2 %collective-permute-done.15.refs_14_ = bf16[256,512]{1,0:T(8,128)(2,1)S(1)} collective-permute-done((bf16[256,512]{1,0:T(8,128)(2,1)S(1)}, bf16[256,512]{1,0:T(8,128)(2,1)S(1)}, u32[]{:S(2)}, u32[]{:S(2)}) %collective-permute-start.15) | collective-permute-done | bytes 262176 | tf_op jit(solution)/shard_map/ppermute | solution.py:605
  101.0 0.5 collective-permute-start.17
  101.5 2.3 collective-permute-done.4.refs_21_
  103.8 10.5 %collective-permute-done.5.refs_22_ = bf16[128,512]{1,0:T(8,128)(2,1)S(1)} collective-permute-done((bf16[128,512]{1,0:T(8,128)(2,1)S(1)}, bf16[128,512]{1,0:T(8,128)(2,1)S(1)}, u32[]{:S(2)}, u32[]{:S(2)}) %collective-permute-start.5) | collective-permute-done | bytes 131104 | tf_op jit(solution)/shard_map/ppermute | solution.py:605
  114.3 0.5 collective-permute-start.20
  114.8 2.4 %shard_map.147.refs_3_ = bf16[128,1024]{1,0:T(8,128)(2,1)S(1)} custom-call(bf16[128,8192]{1,0:T(8,128)(2,1)S(1)} %get-tuple-element.77.normed, bf16[8192,1536]{1,0:T(8,128)(2,1)S(1)} %copy-done.1, f32[128,128]{1,0:T(8,128)S(1)} %get-tuple-element.74.refs_4_.cosine, f32[128,128]{1,0:T(8,128)S(1)} %get-tuple-element.75.refs_5_.sine), custom_call_target="tpu_custom_call" | custom-call | flops 4294967296 | bytes 4194304 | tf_op jit(solution)/shard_map/pallas_call | solution.py:183
  117.3 10.3 %shard_map.148.weight = bf16[1024,8192]{1,0:T(8,128)(2,1)S(1)} custom-call(bf16[1024,8192]{1,0:T(8,128)(2,1)} %stored.1, f32[8,64]{1,0:T(8,128)S(1)} %copy-done.4), custom_call_target="tpu_custom_call" | custom-call | flops 67108864 | bytes 16777216 | tf_op jit(solution)/shard_map/pallas_call | solution.py:222
  127.6 7.0 %shard_map.153 = f32[1024,128]{1,0:T(8,128)S(1)} custom-call(bf16[1024,8192]{1,0:T(8,128)(2,1)S(1)} %shard_map.148.weight, f32[1,8192]{1,0:T(1,128)S(1)} %bitcast.29), custom_call_target="tpu_custom_call" | custom-call | flops 67108864 | bytes 16777216 | tf_op jit(solution)/shard_map/pallas_call | solution.py:250
  134.6 0.5 collective-permute-start.22
  135.2 0.4 collective-permute-start.24
  136.6 19.5 %shard_map.149.attended = bf16[512,1024]{1,0:T(8,128)(2,1)S(1)} custom-call(s32[14]{0:T(128)S(1)} %pad_add_fusion.1.refs_0_, bf16[128,1024]{1,0:T(8,128)(2,1)S(1)} %shard_map.142.refs_1_, bf16[256,1024]{1,0:T(8,128)(2,1)S(1)} %shard_map.145.refs_2_, bf16[128,1024]{1,0:T(8,128)(2,1)S(1)} %shard_map.147.refs_3_, ...), custom_call_target="tpu_custom_call" | custom-call | flops 4294967296 | bytes 8388608 | tf_op jit(solution)/shard_map/pallas_call | solution.py:409
  156.1 2.4 %shard_map.150 = (bf16[256,2048]{1,0:T(8,128)(2,1)S(1)}, bf16[256,2048]{1,0:T(8,128)(2,1)S(1)}) custom-call(bf16[512,1024]{1,0:T(8,128)(2,1)S(1)} %shard_map.149.attended, bf16[1024,8192]{1,0:T(8,128)(2,1)S(1)} %shard_map.148.weight), custom_call_target="tpu_custom_call" | custom-call | flops 4294967296 | bytes 2097152 | tf_op jit(solution)/shard_map/pallas_call | solution.py:451
  158.5 0.7 collective-permute-start.27
  159.2 1.5 collective-permute-start.28
  160.7 2.4 %shard_map.151 = (bf16[256,2048]{1,0:T(8,128)(2,1)S(1)}, bf16[256,2048]{1,0:T(8,128)(2,1)S(1)}) custom-call(bf16[512,1024]{1,0:T(8,128)(2,1)S(1)} %shard_map.149.attended, bf16[1024,8192]{1,0:T(8,128)(2,1)S(1)} %shard_map.148.weight), custom_call_target="tpu_custom_call" | custom-call | flops 4294967296 | bytes 2097152 | tf_op jit(solution)/shard_map/pallas_call | solution.py:451
  163.1 1.6 collective-permute-start.25
  164.7 0.5 collective-permute-start.26
  165.6 3.2 %collective-permute-start.29 = (f32[4]{0:T(128)S(1)}, f32[4]{0:T(128)S(1)}, u32[]{:S(2)}, u32[]{:S(2)}) collective-permute-start(f32[4]{0:T(128)S(1)} %select_reduce_fusion), channel_id=1, source_target_pairs={{0,4},{4,0},{8,12},{12,8},{16,20},{20,16},{24,28},{28,24},{1,5},{5... | collective-permute-start | bytes 56 | tf_op jit(solution)/shard_map/ppermute | solution.py:675
  168.7 4.7 %shard_map.152 = (bf16[128,8192]{1,0:T(8,128)(2,1)S(1)}, bf16[128,8192]{1,0:T(8,128)(2,1)S(1)}) custom-call(bf16[512,1024]{1,0:T(8,128)(2,1)S(1)} %shard_map.149.attended, bf16[1024,8192]{1,0:T(8,128)(2,1)S(1)} %shard_map.148.weight), custom_call_target="tpu_custom_call" | custom-call | flops 8589934592 | bytes 4194304 | tf_op jit(solution)/shard_map/pallas_call | solution.py:478
  173.5 3.5 %collective-permute-done.30 = f32[4]{0:T(128)S(1)} collective-permute-done((f32[4]{0:T(128)S(1)}, f32[4]{0:T(128)S(1)}, u32[]{:S(2)}, u32[]{:S(2)}) %collective-permute-start.30) | collective-permute-done | bytes 48 | tf_op jit(solution)/shard_map/ppermute | solution.py:675
  177.1 4.4 %collective-permute-done.31 = f32[4]{0:T(128)S(1)} collective-permute-done((f32[4]{0:T(128)S(1)}, f32[4]{0:T(128)S(1)}, u32[]{:S(2)}, u32[]{:S(2)}) %collective-permute-start.31) | collective-permute-done | bytes 48 | tf_op jit(solution)/shard_map/ppermute | solution.py:675
  181.5 0.7 collective-permute-done.28.near_y
  182.6 1.5 collective-permute-start.35
  184.1 1.5 collective-permute-start.36
  185.6 0.5 collective-permute-start.32
  186.1 29.0 %collective-permute-done.32 = f32[4]{0:T(128)S(1)} collective-permute-done((f32[4]{0:T(128)S(1)}, f32[4]{0:T(128)S(1)}, u32[]{:S(2)}, u32[]{:S(2)}) %collective-permute-start.32) | collective-permute-done | bytes 48 | tf_op jit(solution)/shard_map/ppermute | solution.py:582
  215.1 0.4 add_convert_fusion
  215.5 1.6 collective-permute-start.33
  217.1 0.5 collective-permute-start.34
  217.6 0.6 collective-permute-start.37
  218.2 10.0 %collective-permute-done.37 = f32[4]{0:T(128)S(1)} collective-permute-done((f32[4]{0:T(128)S(1)}, f32[4]{0:T(128)S(1)}, u32[]{:S(2)}, u32[]{:S(2)}) %collective-permute-start.37) | collective-permute-done | bytes 48 | tf_op jit(solution)/shard_map/ppermute | solution.py:582
  228.2 0.5 convert_divide_fusion
  228.7 2.2 shard_map.154.rest_0_
  230.9 2.2 shard_map.155
  (80 shorter events, 3.9 us)
Async XLA Ops:
  0.6 12.5 %copy-start.2 = (bf16[128,8192]{1,0:T(8,128)(2,1)S(1)}, bf16[128,8192]{1,0:T(8,128)(2,1)}, u32[]{:S(2)}) copy-start(bf16[128,8192]{1,0:T(8,128)(2,1)} %token_.3) | copy-start | bytes 6291460
  0.6 57.9 %collective-permute-start = (bf16[128,8192]{1,0:T(8,128)(2,1)}, bf16[128,8192]{1,0:T(8,128)(2,1)}, u32[]{:S(2)}, u32[]{:S(2)}) collective-permute-start(bf16[128,8192]{1,0:T(8,128)(2,1)} %token_.3), channel_id=1, source_target_pairs={{0,1},{1,0},{2,3},{3,2},{4,5},{5,4},{6,7},{7,6},{8,9},{9,8},{10,11... | collective-permute-start | bytes 6291464 | tf_op jit(solution)/shard_map/ppermute | solution.py:582
  3.6 54.9 %collective-permute-start.1 = (bf16[128,8192]{1,0:T(8,128)(2,1)}, bf16[128,8192]{1,0:T(8,128)(2,1)}, u32[]{:S(2)}, u32[]{:S(2)}) collective-permute-start(bf16[128,8192]{1,0:T(8,128)(2,1)} %token_.3), channel_id=1, source_target_pairs={{0,2},{1,3},{2,0},{3,1},{4,6},{5,7},{6,4},{7,5},{8,10},{9,11},{10,... | collective-permute-start | bytes 6291464 | tf_op jit(solution)/shard_map/ppermute | solution.py:582
  12.7 1.1 copy-start.6
  12.7 1.2 copy-start.7
  12.7 1.3 copy-start.5
  14.0 25.4 %copy-start.3 = (f32[8192]{0:T(1024)S(1)}, f32[8192]{0:T(1024)}, u32[]{:S(2)}) copy-start(f32[8192]{0:T(1024)} %param.14) | copy-start | bytes 98308
  31.1 8.3 %copy-start = (bf16[8192,1536]{1,0:T(8,128)(2,1)}, bf16[8192,1536]{1,0:T(8,128)(2,1)S(1)}, u32[]{:S(2)}) copy-start(bf16[8192,1536]{1,0:T(8,128)(2,1)S(1)} %shard_map.140.refs_3_.weight.refs_5_) | copy-start | bytes 75497472
  39.5 8.2 %copy-start.1 = (bf16[8192,1536]{1,0:T(8,128)(2,1)S(1)}, bf16[8192,1536]{1,0:T(8,128)(2,1)}, u32[]{:S(2)}) copy-start(bf16[8192,1536]{1,0:T(8,128)(2,1)} %copy-done) | copy-start | bytes 75497472
  50.5 19.0 %collective-permute-start.7 = (bf16[128,512]{1,0:T(8,128)(2,1)S(1)}, bf16[128,512]{1,0:T(8,128)(2,1)S(1)}, u32[]{:S(2)}, u32[]{:S(2)}) collective-permute-start(bf16[128,512]{1,0:T(8,128)(2,1)S(1)} %get-tuple-element.81.refs_4_), channel_id=1, source_target_pairs={{0,8},{4,12},{8,16},{12,20},{16,24},{20,28},{24,0},{28,4},{1,9},{5... | collective-permute-start | bytes 393224 | tf_op jit(solution)/shard_map/ppermute | solution.py:605
  52.1 17.5 %collective-permute-start.8 = (bf16[128,512]{1,0:T(8,128)(2,1)S(1)}, bf16[128,512]{1,0:T(8,128)(2,1)S(1)}, u32[]{:S(2)}, u32[]{:S(2)}) collective-permute-start(bf16[128,512]{1,0:T(8,128)(2,1)S(1)} %get-tuple-element.81.refs_4_), channel_id=1, source_target_pairs={{0,16},{4,20},{8,24},{12,28},{16,0},{20,4},{24,8},{28,12},{1,17},{... | collective-permute-start | bytes 393224 | tf_op jit(solution)/shard_map/ppermute | solution.py:605
  54.7 30.3 %collective-permute-start.9 = (bf16[128,512]{1,0:T(8,128)(2,1)S(1)}, bf16[128,512]{1,0:T(8,128)(2,1)S(1)}, u32[]{:S(2)}, u32[]{:S(2)}) collective-permute-start(bf16[128,512]{1,0:T(8,128)(2,1)S(1)} %get-tuple-element.81.refs_4_), channel_id=1, source_target_pairs={{0,24},{4,28},{8,0},{12,4},{16,8},{20,12},{24,16},{28,20},{1,25},{... | collective-permute-start | bytes 393224 | tf_op jit(solution)/shard_map/ppermute | solution.py:605
  61.0 23.6 %collective-permute-start.2 = (bf16[128,4096]{1,0:T(8,128)(2,1)S(1)}, bf16[128,4096]{1,0:T(8,128)(2,1)S(1)}, u32[]{:S(2)}, u32[]{:S(2)}) collective-permute-start(bf16[128,4096]{1,0:T(8,128)(2,1)S(1)} %get-tuple-element.64), channel_id=1, source_target_pairs={{0,2},{1,3},{2,0},{3,1},{4,6},{5,7},{6,4},{7,5},{8,10},{9,11},{10,... | collective-permute-start | bytes 3145736 | tf_op jit(solution)/shard_map/ppermute | solution.py:582
  61.6 23.2 %collective-permute-start.3 = (bf16[128,4096]{1,0:T(8,128)(2,1)S(1)}, bf16[128,4096]{1,0:T(8,128)(2,1)S(1)}, u32[]{:S(2)}, u32[]{:S(2)}) collective-permute-start(bf16[128,4096]{1,0:T(8,128)(2,1)S(1)} %get-tuple-element.65), channel_id=1, source_target_pairs={{0,1},{1,0},{2,3},{3,2},{4,5},{5,4},{6,7},{7,6},{8,9},{9,8},{10,11... | collective-permute-start | bytes 3145736 | tf_op jit(solution)/shard_map/ppermute | solution.py:582
  69.5 16.0 %collective-permute-start.10 = (bf16[128,512]{1,0:T(8,128)(2,1)S(1)}, bf16[128,512]{1,0:T(8,128)(2,1)S(1)}, u32[]{:S(2)}, u32[]{:S(2)}) collective-permute-start(bf16[128,512]{1,0:T(8,128)(2,1)S(1)} %get-tuple-element.81.refs_4_), channel_id=1, source_target_pairs={{0,4},{4,0},{8,12},{12,8},{16,20},{20,16},{24,28},{28,24},{1,5},{5... | collective-permute-start | bytes 393224 | tf_op jit(solution)/shard_map/ppermute | solution.py:611
  69.6 23.2 %collective-permute-start.14 = (bf16[256,512]{1,0:T(8,128)(2,1)S(1)}, bf16[256,512]{1,0:T(8,128)(2,1)S(1)}, u32[]{:S(2)}, u32[]{:S(2)}) collective-permute-start(bf16[256,512]{1,0:T(8,128)(2,1)S(1)} %get-tuple-element.82.refs_12_), channel_id=1, source_target_pairs={{0,8},{4,12},{8,16},{12,20},{16,24},{20,28},{24,0},{28,4},{1,9},{5... | collective-permute-start | bytes 786440 | tf_op jit(solution)/shard_map/ppermute | solution.py:605
  84.6 6.3 %collective-permute-start.11 = (bf16[128,512]{1,0:T(8,128)(2,1)S(1)}, bf16[128,512]{1,0:T(8,128)(2,1)S(1)}, u32[]{:S(2)}, u32[]{:S(2)}) collective-permute-start(bf16[128,512]{1,0:T(8,128)(2,1)S(1)} %collective-permute-done.7.refs_5_), channel_id=1, source_target_pairs={{0,4},{4,0},{8,12},{12,8},{16,20},{20,16},{24,28},{28,24},{1,5},{5... | collective-permute-start | bytes 393224 | tf_op jit(solution)/shard_map/ppermute | solution.py:611
  84.8 6.2 %collective-permute-start.12 = (bf16[128,512]{1,0:T(8,128)(2,1)S(1)}, bf16[128,512]{1,0:T(8,128)(2,1)S(1)}, u32[]{:S(2)}, u32[]{:S(2)}) collective-permute-start(bf16[128,512]{1,0:T(8,128)(2,1)S(1)} %collective-permute-done.8.refs_6_), channel_id=1, source_target_pairs={{0,4},{4,0},{8,12},{12,8},{16,20},{20,16},{24,28},{28,24},{1,5},{5... | collective-permute-start | bytes 393224 | tf_op jit(solution)/shard_map/ppermute | solution.py:611
  85.1 15.9 %collective-permute-start.15 = (bf16[256,512]{1,0:T(8,128)(2,1)S(1)}, bf16[256,512]{1,0:T(8,128)(2,1)S(1)}, u32[]{:S(2)}, u32[]{:S(2)}) collective-permute-start(bf16[256,512]{1,0:T(8,128)(2,1)S(1)} %get-tuple-element.82.refs_12_), channel_id=1, source_target_pairs={{0,16},{4,20},{8,24},{12,28},{16,0},{20,4},{24,8},{28,12},{1,17},{... | collective-permute-start | bytes 786440 | tf_op jit(solution)/shard_map/ppermute | solution.py:605
  85.6 15.5 %collective-permute-start.16 = (bf16[256,512]{1,0:T(8,128)(2,1)S(1)}, bf16[256,512]{1,0:T(8,128)(2,1)S(1)}, u32[]{:S(2)}, u32[]{:S(2)}) collective-permute-start(bf16[256,512]{1,0:T(8,128)(2,1)S(1)} %get-tuple-element.82.refs_12_), channel_id=1, source_target_pairs={{0,24},{4,28},{8,0},{12,4},{16,8},{20,12},{24,16},{28,20},{1,25},{... | collective-permute-start | bytes 786440 | tf_op jit(solution)/shard_map/ppermute | solution.py:605
  90.9 12.9 %collective-permute-start.4 = (bf16[128,512]{1,0:T(8,128)(2,1)S(1)}, bf16[128,512]{1,0:T(8,128)(2,1)S(1)}, u32[]{:S(2)}, u32[]{:S(2)}) collective-permute-start(bf16[128,512]{1,0:T(8,128)(2,1)S(1)} %get-tuple-element.83.refs_20_), channel_id=1, source_target_pairs={{0,8},{4,12},{8,16},{12,20},{16,24},{20,28},{24,0},{28,4},{1,9},{5... | collective-permute-start | bytes 393224 | tf_op jit(solution)/shard_map/ppermute | solution.py:605
  91.0 23.4 %collective-permute-start.5 = (bf16[128,512]{1,0:T(8,128)(2,1)S(1)}, bf16[128,512]{1,0:T(8,128)(2,1)S(1)}, u32[]{:S(2)}, u32[]{:S(2)}) collective-permute-start(bf16[128,512]{1,0:T(8,128)(2,1)S(1)} %get-tuple-element.83.refs_20_), channel_id=1, source_target_pairs={{0,16},{4,20},{8,24},{12,28},{16,0},{20,4},{24,8},{28,12},{1,17},{... | collective-permute-start | bytes 393224 | tf_op jit(solution)/shard_map/ppermute | solution.py:605
  92.9 21.5 %collective-permute-start.6 = (bf16[128,512]{1,0:T(8,128)(2,1)S(1)}, bf16[128,512]{1,0:T(8,128)(2,1)S(1)}, u32[]{:S(2)}, u32[]{:S(2)}) collective-permute-start(bf16[128,512]{1,0:T(8,128)(2,1)S(1)} %get-tuple-element.83.refs_20_), channel_id=1, source_target_pairs={{0,24},{4,28},{8,0},{12,4},{16,8},{20,12},{24,16},{28,20},{1,25},{... | collective-permute-start | bytes 393224 | tf_op jit(solution)/shard_map/ppermute | solution.py:605
  101.0 33.5 %collective-permute-start.13 = (bf16[128,512]{1,0:T(8,128)(2,1)S(1)}, bf16[128,512]{1,0:T(8,128)(2,1)S(1)}, u32[]{:S(2)}, u32[]{:S(2)}) collective-permute-start(bf16[128,512]{1,0:T(8,128)(2,1)S(1)} %collective-permute-done.9.refs_7_), channel_id=1, source_target_pairs={{0,4},{4,0},{8,12},{12,8},{16,20},{20,16},{24,28},{28,24},{1,5},{5... | collective-permute-start | bytes 393224 | tf_op jit(solution)/shard_map/ppermute | solution.py:611
  101.0 33.6 %collective-permute-start.17 = (bf16[256,512]{1,0:T(8,128)(2,1)S(1)}, bf16[256,512]{1,0:T(8,128)(2,1)S(1)}, u32[]{:S(2)}, u32[]{:S(2)}) collective-permute-start(bf16[256,512]{1,0:T(8,128)(2,1)S(1)} %get-tuple-element.82.refs_12_), channel_id=1, source_target_pairs={{0,4},{4,0},{8,12},{12,8},{16,20},{20,16},{24,28},{28,24},{1,5},{5... | collective-permute-start | bytes 786440 | tf_op jit(solution)/shard_map/ppermute | solution.py:611
  103.8 31.3 %collective-permute-start.18 = (bf16[256,512]{1,0:T(8,128)(2,1)S(1)}, bf16[256,512]{1,0:T(8,128)(2,1)S(1)}, u32[]{:S(2)}, u32[]{:S(2)}) collective-permute-start(bf16[256,512]{1,0:T(8,128)(2,1)S(1)} %collective-permute-done.14.refs_13_), channel_id=1, source_target_pairs={{0,4},{4,0},{8,12},{12,8},{16,20},{20,16},{24,28},{28,24},{1,5},{5... | collective-permute-start | bytes 786440 | tf_op jit(solution)/shard_map/ppermute | solution.py:611
  114.3 20.8 %collective-permute-start.19 = (bf16[256,512]{1,0:T(8,128)(2,1)S(1)}, bf16[256,512]{1,0:T(8,128)(2,1)S(1)}, u32[]{:S(2)}, u32[]{:S(2)}) collective-permute-start(bf16[256,512]{1,0:T(8,128)(2,1)S(1)} %collective-permute-done.15.refs_14_), channel_id=1, source_target_pairs={{0,4},{4,0},{8,12},{12,8},{16,20},{20,16},{24,28},{28,24},{1,5},{5... | collective-permute-start | bytes 786440 | tf_op jit(solution)/shard_map/ppermute | solution.py:611
  114.3 21.5 %collective-permute-start.20 = (bf16[256,512]{1,0:T(8,128)(2,1)S(1)}, bf16[256,512]{1,0:T(8,128)(2,1)S(1)}, u32[]{:S(2)}, u32[]{:S(2)}) collective-permute-start(bf16[256,512]{1,0:T(8,128)(2,1)S(1)} %collective-permute-done.16.refs_15_), channel_id=1, source_target_pairs={{0,4},{4,0},{8,12},{12,8},{16,20},{20,16},{24,28},{28,24},{1,5},{5... | collective-permute-start | bytes 786440 | tf_op jit(solution)/shard_map/ppermute | solution.py:611
  114.8 2.5 %copy-start.4 = (f32[8,64]{1,0:T(8,128)S(1)}, f32[8,64]{1,0:T(8,128)}, u32[]{:S(2)}) copy-start(f32[8,64]{1,0:T(8,128)} %scales) | copy-start | bytes 6148
  134.6 1.4 collective-permute-start.21
  134.6 1.5 collective-permute-start.22
  135.1 1.3 collective-permute-start.23
  135.2 1.4 collective-permute-start.24
  158.5 23.0 %collective-permute-start.27 = (bf16[256,2048]{1,0:T(8,128)(2,1)S(1)}, bf16[256,2048]{1,0:T(8,128)(2,1)S(1)}, u32[]{:S(2)}, u32[]{:S(2)}) collective-permute-start(bf16[256,2048]{1,0:T(8,128)(2,1)S(1)} %get-tuple-element.88), channel_id=1, source_target_pairs={{0,1},{1,0},{2,3},{3,2},{4,5},{5,4},{6,7},{7,6},{8,9},{9,8},{10,11... | collective-permute-start | bytes 3145736 | tf_op jit(solution)/shard_map/ppermute | solution.py:582
  159.2 23.0 %collective-permute-start.28 = (bf16[256,2048]{1,0:T(8,128)(2,1)S(1)}, bf16[256,2048]{1,0:T(8,128)(2,1)S(1)}, u32[]{:S(2)}, u32[]{:S(2)}) collective-permute-start(bf16[256,2048]{1,0:T(8,128)(2,1)S(1)} %get-tuple-element.89), channel_id=1, source_target_pairs={{0,2},{1,3},{2,0},{3,1},{4,6},{5,7},{6,4},{7,5},{8,10},{9,11},{10,... | collective-permute-start | bytes 3145736 | tf_op jit(solution)/shard_map/ppermute | solution.py:582
  163.1 52.0 %collective-permute-start.25 = (bf16[256,2048]{1,0:T(8,128)(2,1)S(1)}, bf16[256,2048]{1,0:T(8,128)(2,1)S(1)}, u32[]{:S(2)}, u32[]{:S(2)}) collective-permute-start(bf16[256,2048]{1,0:T(8,128)(2,1)S(1)} %get-tuple-element.91), channel_id=1, source_target_pairs={{0,1},{1,0},{2,3},{3,2},{4,5},{5,4},{6,7},{7,6},{8,9},{9,8},{10,11... | collective-permute-start | bytes 3145736 | tf_op jit(solution)/shard_map/ppermute | solution.py:582
  164.7 50.4 %collective-permute-start.26 = (bf16[256,2048]{1,0:T(8,128)(2,1)S(1)}, bf16[256,2048]{1,0:T(8,128)(2,1)S(1)}, u32[]{:S(2)}, u32[]{:S(2)}) collective-permute-start(bf16[256,2048]{1,0:T(8,128)(2,1)S(1)} %get-tuple-element.92), channel_id=1, source_target_pairs={{0,2},{1,3},{2,0},{3,1},{4,6},{5,7},{6,4},{7,5},{8,10},{9,11},{10,... | collective-permute-start | bytes 3145736 | tf_op jit(solution)/shard_map/ppermute | solution.py:582
  165.6 7.9 %collective-permute-start.29 = (f32[4]{0:T(128)S(1)}, f32[4]{0:T(128)S(1)}, u32[]{:S(2)}, u32[]{:S(2)}) collective-permute-start(f32[4]{0:T(128)S(1)} %select_reduce_fusion), channel_id=1, source_target_pairs={{0,4},{4,0},{8,12},{12,8},{16,20},{20,16},{24,28},{28,24},{1,5},{5... | collective-permute-start | bytes 56 | tf_op jit(solution)/shard_map/ppermute | solution.py:675
  173.5 3.6 %collective-permute-start.30 = (f32[4]{0:T(128)S(1)}, f32[4]{0:T(128)S(1)}, u32[]{:S(2)}, u32[]{:S(2)}) collective-permute-start(f32[4]{0:T(128)S(1)} %add.142), channel_id=1, source_target_pairs={{0,8},{4,12},{8,0},{12,4},{16,24},{20,28},{24,16},{28,20},{1,9},{5... | collective-permute-start | bytes 56 | tf_op jit(solution)/shard_map/ppermute | solution.py:675
  177.1 4.4 %collective-permute-start.31 = (f32[4]{0:T(128)S(1)}, f32[4]{0:T(128)S(1)}, u32[]{:S(2)}, u32[]{:S(2)}) collective-permute-start(f32[4]{0:T(128)S(1)} %add.143), channel_id=1, source_target_pairs={{0,16},{4,20},{8,24},{12,28},{16,0},{20,4},{24,8},{28,12},{1,17},{... | collective-permute-start | bytes 56 | tf_op jit(solution)/shard_map/ppermute | solution.py:675
  182.6 46.1 %collective-permute-start.35 = (bf16[128,2048]{1,0:T(8,128)(2,1)S(1)}, bf16[128,2048]{1,0:T(8,128)(2,1)S(1)}, u32[]{:S(2)}, u32[]{:S(2)}) collective-permute-start(bf16[128,2048]{1,0:T(8,128)(2,1)S(1)} %get-tuple-element.117), channel_id=1, source_target_pairs={{0,2},{1,3},{2,0},{3,1},{4,6},{5,7},{6,4},{7,5},{8,10},{9,11},{10,... | collective-permute-start | bytes 1572872 | tf_op jit(solution)/shard_map/ppermute | solution.py:582
  184.1 44.6 %collective-permute-start.36 = (bf16[128,2048]{1,0:T(8,128)(2,1)S(1)}, bf16[128,2048]{1,0:T(8,128)(2,1)S(1)}, u32[]{:S(2)}, u32[]{:S(2)}) collective-permute-start(bf16[128,2048]{1,0:T(8,128)(2,1)S(1)} %get-tuple-element.116), channel_id=1, source_target_pairs={{0,1},{1,0},{2,3},{3,2},{4,5},{5,4},{6,7},{7,6},{8,9},{9,8},{10,11... | collective-permute-start | bytes 1572872 | tf_op jit(solution)/shard_map/ppermute | solution.py:582
  185.6 29.5 %collective-permute-start.32 = (f32[4]{0:T(128)S(1)}, f32[4]{0:T(128)S(1)}, u32[]{:S(2)}, u32[]{:S(2)}) collective-permute-start(f32[4]{0:T(128)S(1)} %add.144), channel_id=1, source_target_pairs={{0,1},{1,0},{2,3},{3,2},{4,5},{5,4},{6,7},{7,6},{8,9},{9,8},{10,11... | collective-permute-start | bytes 56 | tf_op jit(solution)/shard_map/ppermute | solution.py:582
  215.5 15.4 %collective-permute-start.33 = (bf16[128,2048]{1,0:T(8,128)(2,1)S(1)}, bf16[128,2048]{1,0:T(8,128)(2,1)S(1)}, u32[]{:S(2)}, u32[]{:S(2)}) collective-permute-start(bf16[128,2048]{1,0:T(8,128)(2,1)S(1)} %get-tuple-element.115), channel_id=1, source_target_pairs={{0,2},{1,3},{2,0},{3,1},{4,6},{5,7},{6,4},{7,5},{8,10},{9,11},{10,... | collective-permute-start | bytes 1572872 | tf_op jit(solution)/shard_map/ppermute | solution.py:582
  217.1 13.8 %collective-permute-start.34 = (bf16[128,2048]{1,0:T(8,128)(2,1)S(1)}, bf16[128,2048]{1,0:T(8,128)(2,1)S(1)}, u32[]{:S(2)}, u32[]{:S(2)}) collective-permute-start(bf16[128,2048]{1,0:T(8,128)(2,1)S(1)} %get-tuple-element.114), channel_id=1, source_target_pairs={{0,1},{1,0},{2,3},{3,2},{4,5},{5,4},{6,7},{7,6},{8,9},{9,8},{10,11... | collective-permute-start | bytes 1572872 | tf_op jit(solution)/shard_map/ppermute | solution.py:582
  217.6 10.6 %collective-permute-start.37 = (f32[4]{0:T(128)S(1)}, f32[4]{0:T(128)S(1)}, u32[]{:S(2)}, u32[]{:S(2)}) collective-permute-start(f32[4]{0:T(128)S(1)} %add.147), channel_id=1, source_target_pairs={{0,2},{1,3},{2,0},{3,1},{4,6},{5,7},{6,4},{7,5},{8,10},{9,11},{10,... | collective-permute-start | bytes 56 | tf_op jit(solution)/shard_map/ppermute | solution.py:582

commit v2 on v1

--- a/solution.py
+++ b/solution.py
@@ -140,7 +140,7 @@
         out_shape=VMEM((width, sum(widths)), BF16),
         scratch_shapes=[VMEM((2, depth, one), BF16) for one in widths]
         + [pltpu.SemaphoreType.DMA((len(widths), 2))],
-        compiler_params=params(16),
+        compiler_params=params(6),
         cost_estimate=cost(600 * width * sum(widths), 2 * width * sum(widths)),
     )(*[outside(one) for one in stored], *scales)
 
@@ -167,7 +167,7 @@
             jax.ShapeDtypeStruct((total, width), BF16),
             jax.ShapeDtypeStruct((total, 2 * key_cols), BF16),
         ],
-        compiler_params=params(16),
+        compiler_params=params(6),
         cost_estimate=cost(8 * total * width * key_cols, 6 * total * width),
     )(*[one for one, _ in parts], gain, resident(weight), cosine, sine)
 
@@ -185,7 +185,7 @@
         in_specs=[inside] * 4,
         out_specs=inside,
         out_shape=jax.ShapeDtypeStruct((total, columns), BF16),
-        compiler_params=params(16),
+        compiler_params=params(6),
         cost_estimate=cost(4 * total * width * columns, 4 * total * width),
     )(normed, resident(weight), cosine, sine)
 
@@ -225,7 +225,7 @@
         out_specs=pl.BlockSpec(memory_space=VMEM),
         out_shape=VMEM((rows, width), BF16),
         scratch_shapes=[VMEM((2, depth, width), BF16), pltpu.SemaphoreType.DMA((2,))],
-        compiler_params=params(8),
+        compiler_params=params(5),
         cost_estimate=cost(8 * rows * width, 2 * rows * width),
     )(outside(stored), scales)
 
@@ -252,7 +252,7 @@
         in_specs=[inside] * 2,
         out_specs=inside,
         out_shape=jax.ShapeDtypeStruct((rows, BLOCK), F32),
-        compiler_params=params(8),
+        compiler_params=params(5),
         cost_estimate=cost(8 * rows * width, 2 * rows * width),
     )(resident(weight), vector)
 
@@ -274,7 +274,7 @@
         in_specs=[first, second],
         out_specs=[first, first],
         out_shape=[jax.ShapeDtypeStruct((rows, width // 2), BF16)] * 2,
-        compiler_params=params(8),
+        compiler_params=params(5),
         cost_estimate=cost(0, 4 * rows * width),
     )(one, two)
 
@@ -418,7 +418,9 @@
             pltpu.SemaphoreType.DMA((units, blocks)),
             pltpu.SemaphoreType.DMA((len(kinds),)),
         ],
-        compiler_params=params(20),
+        compiler_params=params(
+            3 + 4 * (units * length * kv_heads * HDIM + length * columns) // MIB
+        ),
         cost_estimate=cost(8 * length * columns * 1024, 8 * MIB),
     )(meta, *queries, *held)
 
@@ -648,10 +650,11 @@
     own_query = project_queries(normed, weight, 2 * key_cols, *tables[0])
 
     if square:
-        near[1], near[2], own_query = lax.optimization_barrier((near[1], near[2], own_query))
+        near[1], near[2], held = lax.optimization_barrier((near[1], near[2], held))
         low, high = halves(near[1], near[2])
         far_low, far_high = flip_tp(low, 2), flip_tp(high, 1)
     queries = [own_query]
+    waiting = []
     for flips, table in zip(kinds[1:], tables[1:]):
         if square and flips == (3,):
             far_low, far_high, queries = lax.optimization_barrier((far_low, far_high, queries))
@@ -659,14 +662,13 @@
         else:
             parts = [(near[flip], side) for flip in flips for side in range(2)]
         normed, pair = project_keys(parts, rows, gain, weight, key_cols, *table)
-        along = exchange_along(pair)
-        query = project_queries(normed, weight, 2 * key_cols, *table)
-        if flips == kinds[-1]:
-            query, late_scale = lax.optimization_barrier((query, out_scale))
-            back = dequant_back(w_out, late_scale)
-            along, query, back = lax.optimization_barrier((along, query, back))
+        waiting.append(exchange_along(pair))
+        queries.append(project_queries(normed, weight, 2 * key_cols, *table))
+    queries, late_scale = lax.optimization_barrier((queries, out_scale))
+    back = dequant_back(w_out, late_scale)
+    waiting, queries, back = lax.optimization_barrier((waiting, queries, back))
+    for along in waiting:
         held += exchange_across(along)
-        queries.append(query)
 
     attended = attend(meta, queries, held, n_ctx, rows, kv_heads, group, kinds)
 
@@ -697,7 +699,9 @@
     for part in range(parts):
         out_x, out_y = outward(attended, back, part * span, span)
         sent.append((flip_tp(out_x, 1), flip_tp(out_y, 2)))
-        attended, out_x, out_y = lax.optimization_barrier((attended, out_x, out_y))
+        attended, vector, out_x, out_y = lax.optimization_barrier(
+            (attended, vector, out_x, out_y)
+        )
     inner, term = kept_terms(attended, back)
     partial = span_sums(attended, toward_score(back, vector))
 

time: 235 us -> 205 us (0.87)
  local copies, waits for them, and re-layouts: 20.4 us -> 3.3 us
  waiting for transfers between devices: 77.1 us -> 60.1 us
    unnamed x20 -> x22, local copies, waits for them, and re-layouts: 17.5 us -> 1.06 us
    ppermute x14, waiting for transfers between devices: 49.3 us -> 40.9 us  [flip_tp(): return lax.ppermute(value, 'tp', [(i, i ^ flip) for i in range(n_tp)])]
    ppermute x9, waiting for transfers between devices: 19 us -> 11.1 us  [exchange_along(): lax.ppermute(value, 'ctx', [(i, (i + 2 * step) % n_ctx) for i in range(n_...]
  transfers between devices with their start and end apart: 38 -> 38, of which waited for: 14 -> 10; matrix products, arithmetic and copies ran while one was open for 4% -> 5% of each run, Pallas kernels for 29% -> 33%
where the time goes in v2:
time: 205 us; the launch traced here: 202 us
  Pallas kernels  93.1 us (45%)
  waiting for transfers between devices  60.1 us (29%)
  starting transfers between devices  37.4 us (18%)
  other arithmetic  5.63 us (3%)
  local copies, waits for them, and re-layouts  3.3 us (2%)
    ppermute x14, waiting for transfers between devices, flip_tp(): return lax.ppermute(value, 'tp', [(i, i ^ flip) for i in range(n_tp)])  40.9 us
    pallas_call x1, Pallas kernels, attend(): pl.pallas_call(functools.partial(attend_body, sizes), in_specs=[pl.BlockS...  19.5 us
    pallas_call x1, Pallas kernels, dequant_joint(): pl.pallas_call(functools.partial(joint_body, len(stored)), in_specs=[pl.B...  17.1 us
    ppermute x14, starting transfers between devices, flip_tp(): return lax.ppermute(value, 'tp', [(i, i ^ flip) for i in range(n_tp)])  16.6 us
    ppermute x9, starting transfers between devices, exchange_along(): lax.ppermute(value, 'ctx', [(i, (i + 2 * step) % n_ctx) for i in range(n_...  13.5 us
    pallas_call x3, Pallas kernels, project_keys(): pl.pallas_call(functools.partial(keys_body, blocks), grid=(1,), in_specs=...  13.1 us
    ppermute x9, waiting for transfers between devices, exchange_along(): lax.ppermute(value, 'ctx', [(i, (i + 2 * step) % n_ctx) for i in range(n_...  11.1 us
    pallas_call x1, Pallas kernels, dequant_back(): pl.pallas_call(back_body, in_specs=[pl.BlockSpec(memory_space=HBM), pl.Bl...  10.3 us
  transfers between devices with their start and end apart: 38, of which 10 were waited for; matrix products, arithmetic and copies ran while one was open for 5% of the time, Pallas kernels for 33%

profile of v2, /device:TPU:0, one launch (start us, length us, event | category | flops | bytes accessed | tf_op | source)
XLA Modules:
  0.0 201.8 jit_solution(14322532088987297502)
XLA Ops:
  0.7 3.0 %collective-permute-start.1 = (bf16[128,8192]{1,0:T(8,128)(2,1)}, bf16[128,8192]{1,0:T(8,128)(2,1)}, u32[]{:S(2)}, u32[]{:S(2)}) collective-permute-start(bf16[128,8192]{1,0:T(8,128)(2,1)} %token_.3), channel_id=1, source_target_pairs={{0,2},{1,3},{2,0},{3,1},{4,6},{5,7},{6,4},{7,5},{8,10},{9,11},{10,... | collective-permute-start | bytes 6291464 | tf_op jit(solution)/shard_map/ppermute | solution.py:584
  3.7 1.5 collective-permute-start
  5.2 0.7 broadcast_in_dim.71
  5.9 0.7 reshape.406
  6.7 0.9 convert_reduce_fusion
  7.7 1.2 dynamic_slice.3
  9.6 1.0 fusion.2
  11.0 0.6 gather_fusion
  12.0 0.6 pad_add_fusion.1.refs_0_
  12.9 0.6 convolution_bitcast_fusion
  13.5 17.1 %shard_map.140.refs_3_.refs_5_.weight = bf16[8192,1536]{1,0:T(8,128)(2,1)S(1)} custom-call(bf16[8192,256]{1,0:T(8,128)(2,1)} %refs_0_.2, bf16[8192,256]{1,0:T(8,128)(2,1)} %refs_1_.2, bf16[8192,1024]{1,0:T(8,128)(2,1)} %refs_2_.1, f32[64,2]{1,0:T(8,128)S(1)} %copy.22.refs_3_, f32[64,2]{1,0:T(8,128)S(1)} %copy.23.refs_4_, f32[64,8]{1,0:T(8,128)S(1)} %copy.24.refs_5_), custom_call_target="tpu_custom_call" | custom-call | flops 7549747200 | bytes 25165824 | tf_op jit(solution)/shard_map/pallas_call | solution.py:135
  30.6 2.9 %shard_map.141 = (bf16[128,8192]{1,0:T(8,128)(2,1)S(1)}, bf16[128,512]{1,0:T(8,128)(2,1)S(1)}) custom-call(bf16[128,8192]{1,0:T(8,128)(2,1)S(1)} %copy-done.1, bf16[128,8192]{1,0:T(8,128)(2,1)S(1)} %copy-done.1, f32[1,8192]{1,0:T(1,128)S(1)} %bitcast.26, bf16[8192,1536]{1,0:T(8,128)(2,1)S(1)} %shard_map.140.refs_3_.refs_5_.weight, ...), custom_call_target="tpu_custom_call" | custom-call | flops 2147483648 | bytes 6291456 | tf_op jit(solution)/shard_map/pallas_call | solution.py:160
  33.6 3.7 %collective-permute-start.4 = (bf16[128,512]{1,0:T(8,128)(2,1)S(1)}, bf16[128,512]{1,0:T(8,128)(2,1)S(1)}, u32[]{:S(2)}, u32[]{:S(2)}) collective-permute-start(bf16[128,512]{1,0:T(8,128)(2,1)S(1)} %get-tuple-element.103.refs_4_), channel_id=1, source_target_pairs={{0,24},{4,28},{8,0},{12,4},{16,8},{20,12},{24,16},{28,20},{1,25},{... | collective-permute-start | bytes 393224 | tf_op jit(solution)/shard_map/ppermute | solution.py:607
  37.3 1.0 collective-permute-start.2
  38.3 2.9 %collective-permute-done.4.refs_7_ = bf16[128,512]{1,0:T(8,128)(2,1)S(1)} collective-permute-done((bf16[128,512]{1,0:T(8,128)(2,1)S(1)}, bf16[128,512]{1,0:T(8,128)(2,1)S(1)}, u32[]{:S(2)}, u32[]{:S(2)}) %collective-permute-start.4) | collective-permute-done | bytes 131104 | tf_op jit(solution)/shard_map/ppermute | solution.py:607
  41.2 8.2 %collective-permute-done.3.refs_6_ = bf16[128,512]{1,0:T(8,128)(2,1)S(1)} collective-permute-done((bf16[128,512]{1,0:T(8,128)(2,1)S(1)}, bf16[128,512]{1,0:T(8,128)(2,1)S(1)}, u32[]{:S(2)}, u32[]{:S(2)}) %collective-permute-start.3) | collective-permute-done | bytes 131104 | tf_op jit(solution)/shard_map/ppermute | solution.py:607
  49.4 0.5 collective-permute-start.6
  49.9 2.4 %shard_map.144.refs_1_ = bf16[128,1024]{1,0:T(8,128)(2,1)S(1)} custom-call(bf16[128,8192]{1,0:T(8,128)(2,1)S(1)} %get-tuple-element.86.normed, bf16[8192,1536]{1,0:T(8,128)(2,1)S(1)} %shard_map.140.refs_3_.refs_5_.weight, f32[128,128]{1,0:T(8,128)S(1)} %get-tuple-element.76.refs_4_.cosine, f32[128,128]{1,0:T(8,128)S(1)} %get-tuple-element.77.refs_5_.sine), custom_call_target="tpu_custom_call" | custom-call | flops 4294967296 | bytes 4194304 | tf_op jit(solution)/shard_map/pallas_call | solution.py:183
  52.4 2.4 %shard_map.143 = (bf16[128,4096]{1,0:T(8,128)(2,1)S(1)}, bf16[128,4096]{1,0:T(8,128)(2,1)S(1)}) custom-call(bf16[128,8192]{1,0:T(8,128)(2,1)} %collective-permute-done.refs_0_.refs_1_.one, bf16[128,8192]{1,0:T(8,128)(2,1)} %collective-permute-done.1.refs_2_.refs_3_.two), custom_call_target="tpu_custom_call" | custom-call | bytes 4194304 | tf_op jit(solution)/shard_map/pallas_call | solution.py:271
  54.8 0.6 collective-permute-start.12
  55.4 0.5 collective-permute-start.13
  55.9 7.4 %shard_map.142 = (bf16[256,8192]{1,0:T(8,128)(2,1)S(1)}, bf16[256,512]{1,0:T(8,128)(2,1)S(1)}) custom-call(bf16[128,8192]{1,0:T(8,128)(2,1)} %collective-permute-done.refs_0_.refs_1_.one, bf16[128,8192]{1,0:T(8,128)(2,1)} %collective-permute-done.refs_0_.refs_1_.one, bf16[128,8192]{1,0:T(8,128)(2,1)} %collective-permute-done.1.refs_2_.refs_3_.two, ...), custom_call_target="tpu_custom_call" | custom-call | flops 4294967296 | bytes 12582912 | tf_op jit(solution)/shard_map/pallas_call | solution.py:160
  63.4 3.3 %collective-permute-start.11 = (bf16[256,512]{1,0:T(8,128)(2,1)S(1)}, bf16[256,512]{1,0:T(8,128)(2,1)S(1)}, u32[]{:S(2)}, u32[]{:S(2)}) collective-permute-start(bf16[256,512]{1,0:T(8,128)(2,1)S(1)} %get-tuple-element.111.refs_12_), channel_id=1, source_target_pairs={{0,24},{4,28},{8,0},{12,4},{16,8},{20,12},{24,16},{28,20},{1,25},{... | collective-permute-start | bytes 786440 | tf_op jit(solution)/shard_map/ppermute | solution.py:607
  66.7 1.0 collective-permute-start.9
  67.7 4.6 %shard_map.145.refs_2_ = bf16[256,1024]{1,0:T(8,128)(2,1)S(1)} custom-call(bf16[256,8192]{1,0:T(8,128)(2,1)S(1)} %get-tuple-element.87.normed, bf16[8192,1536]{1,0:T(8,128)(2,1)S(1)} %shard_map.140.refs_3_.refs_5_.weight, f32[256,128]{1,0:T(8,128)S(1)} %fusion.1.refs_6_.cosine, f32[256,128]{1,0:T(8,128)S(1)} %fusion.refs_7_.sine), custom_call_target="tpu_custom_call" | custom-call | flops 8589934592 | bytes 8388608 | tf_op jit(solution)/shard_map/pallas_call | solution.py:183
  72.4 7.6 %collective-permute-done.12.refs_0_ = bf16[128,4096]{1,0:T(8,128)(2,1)S(1)} collective-permute-done((bf16[128,4096]{1,0:T(8,128)(2,1)S(1)}, bf16[128,4096]{1,0:T(8,128)(2,1)S(1)}, u32[]{:S(2)}, u32[]{:S(2)}) %collective-permute-start.12) | collective-permute-done | bytes 1048608 | tf_op jit(solution)/shard_map/ppermute | solution.py:584
  80.2 2.8 %shard_map.146 = (bf16[128,8192]{1,0:T(8,128)(2,1)S(1)}, bf16[128,512]{1,0:T(8,128)(2,1)S(1)}) custom-call(bf16[128,4096]{1,0:T(8,128)(2,1)S(1)} %collective-permute-done.12.refs_0_, bf16[128,4096]{1,0:T(8,128)(2,1)S(1)} %collective-permute-done.13.refs_1_, f32[1,8192]{1,0:T(1,128)S(1)} %bitcast.28, ...), custom_call_target="tpu_custom_call" | custom-call | flops 2147483648 | bytes 6291456 | tf_op jit(solution)/shard_map/pallas_call | solution.py:160
  83.0 1.3 collective-permute-start.16
  84.3 1.2 collective-permute-start.15
  85.5 1.9 collective-permute-start.14
  87.4 2.4 %shard_map.147.refs_3_ = bf16[128,1024]{1,0:T(8,128)(2,1)S(1)} custom-call(bf16[128,8192]{1,0:T(8,128)(2,1)S(1)} %get-tuple-element.95.normed, bf16[8192,1536]{1,0:T(8,128)(2,1)S(1)} %shard_map.140.refs_3_.refs_5_.weight, f32[128,128]{1,0:T(8,128)S(1)} %get-tuple-element.90.refs_4_.cosine, f32[128,128]{1,0:T(8,128)S(1)} %get-tuple-element.91.refs_5_.sine), custom_call_target="tpu_custom_call" | custom-call | flops 4294967296 | bytes 4194304 | tf_op jit(solution)/shard_map/pallas_call | solution.py:183
  89.9 10.3 %shard_map.148.weight = bf16[1024,8192]{1,0:T(8,128)(2,1)S(1)} custom-call(bf16[1024,8192]{1,0:T(8,128)(2,1)} %stored.1, f32[8,64]{1,0:T(8,128)S(1)} %copy-done.4), custom_call_target="tpu_custom_call" | custom-call | flops 67108864 | bytes 16777216 | tf_op jit(solution)/shard_map/pallas_call | solution.py:222
  100.3 0.5 collective-permute-start.22
  100.9 0.4 collective-permute-start.17
  101.4 0.2 collective-permute-done.21.refs_24_
  101.8 0.3 collective-permute-start.20
  102.3 1.5 collective-permute-done.24.refs_27_
  103.8 19.5 %shard_map.149.attended = bf16[512,1024]{1,0:T(8,128)(2,1)S(1)} custom-call(s32[14]{0:T(128)S(1)} %pad_add_fusion.1.refs_0_, bf16[128,1024]{1,0:T(8,128)(2,1)S(1)} %shard_map.144.refs_1_, bf16[256,1024]{1,0:T(8,128)(2,1)S(1)} %shard_map.145.refs_2_, bf16[128,1024]{1,0:T(8,128)(2,1)S(1)} %shard_map.147.refs_3_, ...), custom_call_target="tpu_custom_call" | custom-call | flops 4294967296 | bytes 8388608 | tf_op jit(solution)/shard_map/pallas_call | solution.py:409
  123.4 2.4 %shard_map.150 = (bf16[256,2048]{1,0:T(8,128)(2,1)S(1)}, bf16[256,2048]{1,0:T(8,128)(2,1)S(1)}) custom-call(bf16[512,1024]{1,0:T(8,128)(2,1)S(1)} %shard_map.149.attended, bf16[1024,8192]{1,0:T(8,128)(2,1)S(1)} %shard_map.148.weight), custom_call_target="tpu_custom_call" | custom-call | flops 4294967296 | bytes 2097152 | tf_op jit(solution)/shard_map/pallas_call | solution.py:453
  125.8 1.1 collective-permute-start.27
  127.0 1.5 collective-permute-start.28
  128.5 2.4 %shard_map.151 = (bf16[256,2048]{1,0:T(8,128)(2,1)S(1)}, bf16[256,2048]{1,0:T(8,128)(2,1)S(1)}) custom-call(bf16[512,1024]{1,0:T(8,128)(2,1)S(1)} %shard_map.149.attended, bf16[1024,8192]{1,0:T(8,128)(2,1)S(1)} %shard_map.148.weight), custom_call_target="tpu_custom_call" | custom-call | flops 4294967296 | bytes 2097152 | tf_op jit(solution)/shard_map/pallas_call | solution.py:453
  130.9 1.0 collective-permute-start.25
  131.9 0.5 collective-permute-start.26
  132.4 7.2 %shard_map.153 = f32[1024,128]{1,0:T(8,128)S(1)} custom-call(bf16[1024,8192]{1,0:T(8,128)(2,1)S(1)} %shard_map.148.weight, f32[1,8192]{1,0:T(1,128)S(1)} %bitcast.29), custom_call_target="tpu_custom_call" | custom-call | flops 67108864 | bytes 16777216 | tf_op jit(solution)/shard_map/pallas_call | solution.py:250
  139.8 0.3 multiply_reduce_fusion
  140.2 3.2 %collective-permute-start.29 = (f32[4]{0:T(128)S(1)}, f32[4]{0:T(128)S(1)}, u32[]{:S(2)}, u32[]{:S(2)}) collective-permute-start(f32[4]{0:T(128)S(1)} %select_reduce_fusion), channel_id=1, source_target_pairs={{0,4},{4,0},{8,12},{12,8},{16,20},{20,16},{24,28},{28,24},{1,5},{5... | collective-permute-start | bytes 56 | tf_op jit(solution)/shard_map/ppermute | solution.py:677
  143.4 4.7 %shard_map.152 = (bf16[128,8192]{1,0:T(8,128)(2,1)S(1)}, bf16[128,8192]{1,0:T(8,128)(2,1)S(1)}) custom-call(bf16[512,1024]{1,0:T(8,128)(2,1)S(1)} %shard_map.149.attended, bf16[1024,8192]{1,0:T(8,128)(2,1)S(1)} %shard_map.148.weight), custom_call_target="tpu_custom_call" | custom-call | flops 8589934592 | bytes 4194304 | tf_op jit(solution)/shard_map/pallas_call | solution.py:480
  148.2 3.5 %collective-permute-done.30 = f32[4]{0:T(128)S(1)} collective-permute-done((f32[4]{0:T(128)S(1)}, f32[4]{0:T(128)S(1)}, u32[]{:S(2)}, u32[]{:S(2)}) %collective-permute-start.30) | collective-permute-done | bytes 48 | tf_op jit(solution)/shard_map/ppermute | solution.py:677
  151.7 1.6 collective-permute-start.31
  153.3 2.8 %collective-permute-done.31 = f32[4]{0:T(128)S(1)} collective-permute-done((f32[4]{0:T(128)S(1)}, f32[4]{0:T(128)S(1)}, u32[]{:S(2)}, u32[]{:S(2)}) %collective-permute-start.31) | collective-permute-done | bytes 48 | tf_op jit(solution)/shard_map/ppermute | solution.py:677
  156.2 0.4 add_convert_fusion.2
  156.6 1.1 collective-permute-start.36
  157.7 1.5 collective-permute-start.35
  159.3 0.9 collective-permute-start.32
  160.2 22.2 %collective-permute-done.32 = f32[4]{0:T(128)S(1)} collective-permute-done((f32[4]{0:T(128)S(1)}, f32[4]{0:T(128)S(1)}, u32[]{:S(2)}, u32[]{:S(2)}) %collective-permute-start.32) | collective-permute-done | bytes 48 | tf_op jit(solution)/shard_map/ppermute | solution.py:584
  182.4 0.4 add_convert_fusion
  182.8 1.1 collective-permute-start.34
  183.9 1.5 collective-permute-start.33
  185.5 0.5 collective-permute-start.37
  186.0 10.9 %collective-permute-done.37 = f32[4]{0:T(128)S(1)} collective-permute-done((f32[4]{0:T(128)S(1)}, f32[4]{0:T(128)S(1)}, u32[]{:S(2)}, u32[]{:S(2)}) %collective-permute-start.37) | collective-permute-done | bytes 48 | tf_op jit(solution)/shard_map/ppermute | solution.py:584
  196.8 0.5 convert_divide_fusion
  197.4 2.2 %shard_map.154.rest_0_ = bf16[128,8192]{1,0:T(8,128)(2,1)} custom-call(bf16[128,8192]{1,0:T(8,128)(2,1)S(1)} %copy-done.2, bf16[128,8192]{1,0:T(8,128)(2,1)S(1)} %get-tuple-element.139.term, bf16[256,2048]{1,0:T(8,128)(2,1)S(1)} %collective-permute-done.27.near_x, bf16[256,2048]{1,0:T(8,128)(2,1)S(1)} %collective-permute-done.28.near_y, ...), custom_call_target="tpu_custom_call" | custom-call | flops 262144 | bytes 5242880 | tf_op jit(solution)/shard_map/pallas_call | solution.py:547
  199.6 2.2 %shard_map.155 = bf16[128,8192]{1,0:T(8,128)(2,1)} custom-call(bf16[128,8192]{1,0:T(8,128)(2,1)S(1)} %copy-done.2, bf16[128,8192]{1,0:T(8,128)(2,1)S(1)} %get-tuple-element.139.term, bf16[256,2048]{1,0:T(8,128)(2,1)S(1)} %collective-permute-done.25.near_x, bf16[256,2048]{1,0:T(8,128)(2,1)S(1)} %collective-permute-done.26.near_y, ...), custom_call_target="tpu_custom_call", output_to_operand_aliasing={{}: (6, {})} | custom-call | flops 262144 | bytes 5242880 | tf_op jit(solution)/shard_map/pallas_call | solution.py:547
  (82 shorter events, 2.6 us)
Async XLA Ops:
  0.6 12.2 %copy-start = (bf16[128,8192]{1,0:T(8,128)(2,1)S(1)}, bf16[128,8192]{1,0:T(8,128)(2,1)}, u32[]{:S(2)}) copy-start(bf16[128,8192]{1,0:T(8,128)(2,1)} %token_.3) | copy-start | bytes 6291460
  0.6 10.3 %copy-start.5 = (s32[8]{0:T(128)S(1)}, s32[8]{0:T(128)}, u32[]{:S(2)}) copy-start(s32[8]{0:T(128)} %param.25) | copy-start | bytes 100
  0.7 11.0 %copy-start.6 = (f32[64,8]{0,1:T(8,128)S(1)}, f32[64,8]{0,1:T(8,128)}, u32[]{:S(2)}) copy-start(f32[64,8]{0,1:T(8,128)} %param.16) | copy-start | bytes 6148
  0.7 11.1 %copy-start.7 = (f32[64,2]{0,1:T(2,128)S(1)}, f32[64,2]{0,1:T(2,128)}, u32[]{:S(2)}) copy-start(f32[64,2]{0,1:T(2,128)} %param.18) | copy-start | bytes 1540
  0.7 11.1 %copy-start.8 = (f32[64,2]{0,1:T(2,128)S(1)}, f32[64,2]{0,1:T(2,128)}, u32[]{:S(2)}) copy-start(f32[64,2]{0,1:T(2,128)} %param.20) | copy-start | bytes 1540
  0.7 51.7 %collective-permute-start.1 = (bf16[128,8192]{1,0:T(8,128)(2,1)}, bf16[128,8192]{1,0:T(8,128)(2,1)}, u32[]{:S(2)}, u32[]{:S(2)}) collective-permute-start(bf16[128,8192]{1,0:T(8,128)(2,1)} %token_.3), channel_id=1, source_target_pairs={{0,2},{1,3},{2,0},{3,1},{4,6},{5,7},{6,4},{7,5},{8,10},{9,11},{10,... | collective-permute-start | bytes 6291464 | tf_op jit(solution)/shard_map/ppermute | solution.py:584
  3.7 48.7 %collective-permute-start = (bf16[128,8192]{1,0:T(8,128)(2,1)}, bf16[128,8192]{1,0:T(8,128)(2,1)}, u32[]{:S(2)}, u32[]{:S(2)}) collective-permute-start(bf16[128,8192]{1,0:T(8,128)(2,1)} %token_.3), channel_id=1, source_target_pairs={{0,1},{1,0},{2,3},{3,2},{4,5},{5,4},{6,7},{7,6},{8,9},{9,8},{10,11... | collective-permute-start | bytes 6291464 | tf_op jit(solution)/shard_map/ppermute | solution.py:584
  13.5 17.1 %copy-start.1 = (bf16[128,8192]{1,0:T(8,128)(2,1)S(1)}, bf16[128,8192]{1,0:T(8,128)(2,1)}, u32[]{:S(2)}) copy-start(bf16[128,8192]{1,0:T(8,128)(2,1)} %token_.3) | copy-start | bytes 6291460
  13.5 17.1 %copy-start.3 = (f32[8192]{0:T(1024)S(1)}, f32[8192]{0:T(1024)}, u32[]{:S(2)}) copy-start(f32[8192]{0:T(1024)} %param.14) | copy-start | bytes 98308
  33.5 3.7 %collective-permute-start.5 = (bf16[128,512]{1,0:T(8,128)(2,1)S(1)}, bf16[128,512]{1,0:T(8,128)(2,1)S(1)}, u32[]{:S(2)}, u32[]{:S(2)}) collective-permute-start(bf16[128,512]{1,0:T(8,128)(2,1)S(1)} %get-tuple-element.103.refs_4_), channel_id=1, source_target_pairs={{0,4},{4,0},{8,12},{12,8},{16,20},{20,16},{24,28},{28,24},{1,5},{5... | collective-permute-start | bytes 393224 | tf_op jit(solution)/shard_map/ppermute | solution.py:613
  33.6 7.6 %collective-permute-start.4 = (bf16[128,512]{1,0:T(8,128)(2,1)S(1)}, bf16[128,512]{1,0:T(8,128)(2,1)S(1)}, u32[]{:S(2)}, u32[]{:S(2)}) collective-permute-start(bf16[128,512]{1,0:T(8,128)(2,1)S(1)} %get-tuple-element.103.refs_4_), channel_id=1, source_target_pairs={{0,24},{4,28},{8,0},{12,4},{16,8},{20,12},{24,16},{28,20},{1,25},{... | collective-permute-start | bytes 393224 | tf_op jit(solution)/shard_map/ppermute | solution.py:607
  37.3 12.1 %collective-permute-start.3 = (bf16[128,512]{1,0:T(8,128)(2,1)S(1)}, bf16[128,512]{1,0:T(8,128)(2,1)S(1)}, u32[]{:S(2)}, u32[]{:S(2)}) collective-permute-start(bf16[128,512]{1,0:T(8,128)(2,1)S(1)} %get-tuple-element.103.refs_4_), channel_id=1, source_target_pairs={{0,16},{4,20},{8,24},{12,28},{16,0},{20,4},{24,8},{28,12},{1,17},{... | collective-permute-start | bytes 393224 | tf_op jit(solution)/shard_map/ppermute | solution.py:607
  37.3 12.1 %collective-permute-start.2 = (bf16[128,512]{1,0:T(8,128)(2,1)S(1)}, bf16[128,512]{1,0:T(8,128)(2,1)S(1)}, u32[]{:S(2)}, u32[]{:S(2)}) collective-permute-start(bf16[128,512]{1,0:T(8,128)(2,1)S(1)} %get-tuple-element.103.refs_4_), channel_id=1, source_target_pairs={{0,8},{4,12},{8,16},{12,20},{16,24},{20,28},{24,0},{28,4},{1,9},{5... | collective-permute-start | bytes 393224 | tf_op jit(solution)/shard_map/ppermute | solution.py:607
  41.2 11.1 %collective-permute-start.8 = (bf16[128,512]{1,0:T(8,128)(2,1)S(1)}, bf16[128,512]{1,0:T(8,128)(2,1)S(1)}, u32[]{:S(2)}, u32[]{:S(2)}) collective-permute-start(bf16[128,512]{1,0:T(8,128)(2,1)S(1)} %collective-permute-done.4.refs_7_), channel_id=1, source_target_pairs={{0,4},{4,0},{8,12},{12,8},{16,20},{20,16},{24,28},{28,24},{1,5},{5... | collective-permute-start | bytes 393224 | tf_op jit(solution)/shard_map/ppermute | solution.py:613
  49.4 3.0 %collective-permute-start.7 = (bf16[128,512]{1,0:T(8,128)(2,1)S(1)}, bf16[128,512]{1,0:T(8,128)(2,1)S(1)}, u32[]{:S(2)}, u32[]{:S(2)}) collective-permute-start(bf16[128,512]{1,0:T(8,128)(2,1)S(1)} %collective-permute-done.3.refs_6_), channel_id=1, source_target_pairs={{0,4},{4,0},{8,12},{12,8},{16,20},{20,16},{24,28},{28,24},{1,5},{5... | collective-permute-start | bytes 393224 | tf_op jit(solution)/shard_map/ppermute | solution.py:613
  49.4 3.0 %collective-permute-start.6 = (bf16[128,512]{1,0:T(8,128)(2,1)S(1)}, bf16[128,512]{1,0:T(8,128)(2,1)S(1)}, u32[]{:S(2)}, u32[]{:S(2)}) collective-permute-start(bf16[128,512]{1,0:T(8,128)(2,1)S(1)} %collective-permute-done.2.refs_5_), channel_id=1, source_target_pairs={{0,4},{4,0},{8,12},{12,8},{16,20},{20,16},{24,28},{28,24},{1,5},{5... | collective-permute-start | bytes 393224 | tf_op jit(solution)/shard_map/ppermute | solution.py:613
  54.8 25.1 %collective-permute-start.12 = (bf16[128,4096]{1,0:T(8,128)(2,1)S(1)}, bf16[128,4096]{1,0:T(8,128)(2,1)S(1)}, u32[]{:S(2)}, u32[]{:S(2)}) collective-permute-start(bf16[128,4096]{1,0:T(8,128)(2,1)S(1)} %get-tuple-element.84), channel_id=1, source_target_pairs={{0,2},{1,3},{2,0},{3,1},{4,6},{5,7},{6,4},{7,5},{8,10},{9,11},{10,... | collective-permute-start | bytes 3145736 | tf_op jit(solution)/shard_map/ppermute | solution.py:584
  55.4 24.8 %collective-permute-start.13 = (bf16[128,4096]{1,0:T(8,128)(2,1)S(1)}, bf16[128,4096]{1,0:T(8,128)(2,1)S(1)}, u32[]{:S(2)}, u32[]{:S(2)}) collective-permute-start(bf16[128,4096]{1,0:T(8,128)(2,1)S(1)} %get-tuple-element.85), channel_id=1, source_target_pairs={{0,1},{1,0},{2,3},{3,2},{4,5},{5,4},{6,7},{7,6},{8,9},{9,8},{10,11... | collective-permute-start | bytes 3145736 | tf_op jit(solution)/shard_map/ppermute | solution.py:584
  63.4 22.1 %collective-permute-start.11 = (bf16[256,512]{1,0:T(8,128)(2,1)S(1)}, bf16[256,512]{1,0:T(8,128)(2,1)S(1)}, u32[]{:S(2)}, u32[]{:S(2)}) collective-permute-start(bf16[256,512]{1,0:T(8,128)(2,1)S(1)} %get-tuple-element.111.refs_12_), channel_id=1, source_target_pairs={{0,24},{4,28},{8,0},{12,4},{16,8},{20,12},{24,16},{28,20},{1,25},{... | collective-permute-start | bytes 786440 | tf_op jit(solution)/shard_map/ppermute | solution.py:607
  66.7 33.5 %collective-permute-start.10 = (bf16[256,512]{1,0:T(8,128)(2,1)S(1)}, bf16[256,512]{1,0:T(8,128)(2,1)S(1)}, u32[]{:S(2)}, u32[]{:S(2)}) collective-permute-start(bf16[256,512]{1,0:T(8,128)(2,1)S(1)} %get-tuple-element.111.refs_12_), channel_id=1, source_target_pairs={{0,16},{4,20},{8,24},{12,28},{16,0},{20,4},{24,8},{28,12},{1,17},{... | collective-permute-start | bytes 786440 | tf_op jit(solution)/shard_map/ppermute | solution.py:607
  66.7 33.5 %collective-permute-start.9 = (bf16[256,512]{1,0:T(8,128)(2,1)S(1)}, bf16[256,512]{1,0:T(8,128)(2,1)S(1)}, u32[]{:S(2)}, u32[]{:S(2)}) collective-permute-start(bf16[256,512]{1,0:T(8,128)(2,1)S(1)} %get-tuple-element.111.refs_12_), channel_id=1, source_target_pairs={{0,8},{4,12},{8,16},{12,20},{16,24},{20,28},{24,0},{28,4},{1,9},{5... | collective-permute-start | bytes 786440 | tf_op jit(solution)/shard_map/ppermute | solution.py:607
  83.0 17.2 %collective-permute-start.16 = (bf16[128,512]{1,0:T(8,128)(2,1)S(1)}, bf16[128,512]{1,0:T(8,128)(2,1)S(1)}, u32[]{:S(2)}, u32[]{:S(2)}) collective-permute-start(bf16[128,512]{1,0:T(8,128)(2,1)S(1)} %get-tuple-element.115.refs_20_), channel_id=1, source_target_pairs={{0,24},{4,28},{8,0},{12,4},{16,8},{20,12},{24,16},{28,20},{1,25},{... | collective-permute-start | bytes 393224 | tf_op jit(solution)/shard_map/ppermute | solution.py:607
  84.3 15.9 %collective-permute-start.15 = (bf16[128,512]{1,0:T(8,128)(2,1)S(1)}, bf16[128,512]{1,0:T(8,128)(2,1)S(1)}, u32[]{:S(2)}, u32[]{:S(2)}) collective-permute-start(bf16[128,512]{1,0:T(8,128)(2,1)S(1)} %get-tuple-element.115.refs_20_), channel_id=1, source_target_pairs={{0,16},{4,20},{8,24},{12,28},{16,0},{20,4},{24,8},{28,12},{1,17},{... | collective-permute-start | bytes 393224 | tf_op jit(solution)/shard_map/ppermute | solution.py:607
  85.5 14.7 %collective-permute-start.14 = (bf16[128,512]{1,0:T(8,128)(2,1)S(1)}, bf16[128,512]{1,0:T(8,128)(2,1)S(1)}, u32[]{:S(2)}, u32[]{:S(2)}) collective-permute-start(bf16[128,512]{1,0:T(8,128)(2,1)S(1)} %get-tuple-element.115.refs_20_), channel_id=1, source_target_pairs={{0,8},{4,12},{8,16},{12,20},{16,24},{20,28},{24,0},{28,4},{1,9},{5... | collective-permute-start | bytes 393224 | tf_op jit(solution)/shard_map/ppermute | solution.py:607
  87.4 2.5 %copy-start.4 = (f32[8,64]{1,0:T(8,128)S(1)}, f32[8,64]{1,0:T(8,128)}, u32[]{:S(2)}) copy-start(f32[8,64]{1,0:T(8,128)} %scales) | copy-start | bytes 6148
  100.2 1.4 collective-permute-start.21
  100.3 1.5 collective-permute-start.22
  100.8 1.4 collective-permute-start.23
  100.9 3.0 %collective-permute-start.17 = (bf16[256,512]{1,0:T(8,128)(2,1)S(1)}, bf16[256,512]{1,0:T(8,128)(2,1)S(1)}, u32[]{:S(2)}, u32[]{:S(2)}) collective-permute-start(bf16[256,512]{1,0:T(8,128)(2,1)S(1)} %get-tuple-element.111.refs_12_), channel_id=1, source_target_pairs={{0,4},{4,0},{8,12},{12,8},{16,20},{20,16},{24,28},{28,24},{1,5},{5... | collective-permute-start | bytes 786440 | tf_op jit(solution)/shard_map/ppermute | solution.py:613
  101.3 2.5 %collective-permute-start.18 = (bf16[256,512]{1,0:T(8,128)(2,1)S(1)}, bf16[256,512]{1,0:T(8,128)(2,1)S(1)}, u32[]{:S(2)}, u32[]{:S(2)}) collective-permute-start(bf16[256,512]{1,0:T(8,128)(2,1)S(1)} %collective-permute-done.9.refs_13_), channel_id=1, source_target_pairs={{0,4},{4,0},{8,12},{12,8},{16,20},{20,16},{24,28},{28,24},{1,5},{5... | collective-permute-start | bytes 786440 | tf_op jit(solution)/shard_map/ppermute | solution.py:613
  101.6 2.2 %collective-permute-start.19 = (bf16[256,512]{1,0:T(8,128)(2,1)S(1)}, bf16[256,512]{1,0:T(8,128)(2,1)S(1)}, u32[]{:S(2)}, u32[]{:S(2)}) collective-permute-start(bf16[256,512]{1,0:T(8,128)(2,1)S(1)} %collective-permute-done.10.refs_14_), channel_id=1, source_target_pairs={{0,4},{4,0},{8,12},{12,8},{16,20},{20,16},{24,28},{28,24},{1,5},{5... | collective-permute-start | bytes 786440 | tf_op jit(solution)/shard_map/ppermute | solution.py:613
  101.8 2.0 %collective-permute-start.20 = (bf16[256,512]{1,0:T(8,128)(2,1)S(1)}, bf16[256,512]{1,0:T(8,128)(2,1)S(1)}, u32[]{:S(2)}, u32[]{:S(2)}) collective-permute-start(bf16[256,512]{1,0:T(8,128)(2,1)S(1)} %collective-permute-done.11.refs_15_), channel_id=1, source_target_pairs={{0,4},{4,0},{8,12},{12,8},{16,20},{20,16},{24,28},{28,24},{1,5},{5... | collective-permute-start | bytes 786440 | tf_op jit(solution)/shard_map/ppermute | solution.py:613
  102.1 1.7 collective-permute-start.24
  125.8 30.4 %collective-permute-start.27 = (bf16[256,2048]{1,0:T(8,128)(2,1)S(1)}, bf16[256,2048]{1,0:T(8,128)(2,1)S(1)}, u32[]{:S(2)}, u32[]{:S(2)}) collective-permute-start(bf16[256,2048]{1,0:T(8,128)(2,1)S(1)} %get-tuple-element.121), channel_id=1, source_target_pairs={{0,1},{1,0},{2,3},{3,2},{4,5},{5,4},{6,7},{7,6},{8,9},{9,8},{10,11... | collective-permute-start | bytes 3145736 | tf_op jit(solution)/shard_map/ppermute | solution.py:584
  127.0 29.2 %collective-permute-start.28 = (bf16[256,2048]{1,0:T(8,128)(2,1)S(1)}, bf16[256,2048]{1,0:T(8,128)(2,1)S(1)}, u32[]{:S(2)}, u32[]{:S(2)}) collective-permute-start(bf16[256,2048]{1,0:T(8,128)(2,1)S(1)} %get-tuple-element.122), channel_id=1, source_target_pairs={{0,2},{1,3},{2,0},{3,1},{4,6},{5,7},{6,4},{7,5},{8,10},{9,11},{10,... | collective-permute-start | bytes 3145736 | tf_op jit(solution)/shard_map/ppermute | solution.py:584
  130.9 51.5 %collective-permute-start.25 = (bf16[256,2048]{1,0:T(8,128)(2,1)S(1)}, bf16[256,2048]{1,0:T(8,128)(2,1)S(1)}, u32[]{:S(2)}, u32[]{:S(2)}) collective-permute-start(bf16[256,2048]{1,0:T(8,128)(2,1)S(1)} %get-tuple-element.124), channel_id=1, source_target_pairs={{0,1},{1,0},{2,3},{3,2},{4,5},{5,4},{6,7},{7,6},{8,9},{9,8},{10,11... | collective-permute-start | bytes 3145736 | tf_op jit(solution)/shard_map/ppermute | solution.py:584
  131.9 50.4 %collective-permute-start.26 = (bf16[256,2048]{1,0:T(8,128)(2,1)S(1)}, bf16[256,2048]{1,0:T(8,128)(2,1)S(1)}, u32[]{:S(2)}, u32[]{:S(2)}) collective-permute-start(bf16[256,2048]{1,0:T(8,128)(2,1)S(1)} %get-tuple-element.125), channel_id=1, source_target_pairs={{0,2},{1,3},{2,0},{3,1},{4,6},{5,7},{6,4},{7,5},{8,10},{9,11},{10,... | collective-permute-start | bytes 3145736 | tf_op jit(solution)/shard_map/ppermute | solution.py:584
  140.2 7.9 %collective-permute-start.29 = (f32[4]{0:T(128)S(1)}, f32[4]{0:T(128)S(1)}, u32[]{:S(2)}, u32[]{:S(2)}) collective-permute-start(f32[4]{0:T(128)S(1)} %select_reduce_fusion), channel_id=1, source_target_pairs={{0,4},{4,0},{8,12},{12,8},{16,20},{20,16},{24,28},{28,24},{1,5},{5... | collective-permute-start | bytes 56 | tf_op jit(solution)/shard_map/ppermute | solution.py:677
  148.1 3.6 %collective-permute-start.30 = (f32[4]{0:T(128)S(1)}, f32[4]{0:T(128)S(1)}, u32[]{:S(2)}, u32[]{:S(2)}) collective-permute-start(f32[4]{0:T(128)S(1)} %add.142), channel_id=1, source_target_pairs={{0,8},{4,12},{8,0},{12,4},{16,24},{20,28},{24,16},{28,20},{1,9},{5... | collective-permute-start | bytes 56 | tf_op jit(solution)/shard_map/ppermute | solution.py:677
  151.7 4.4 %collective-permute-start.31 = (f32[4]{0:T(128)S(1)}, f32[4]{0:T(128)S(1)}, u32[]{:S(2)}, u32[]{:S(2)}) collective-permute-start(f32[4]{0:T(128)S(1)} %add.143), channel_id=1, source_target_pairs={{0,16},{4,20},{8,24},{12,28},{16,0},{20,4},{24,8},{28,12},{1,17},{... | collective-permute-start | bytes 56 | tf_op jit(solution)/shard_map/ppermute | solution.py:677
  156.6 40.8 %copy-start.2 = (bf16[128,8192]{1,0:T(8,128)(2,1)S(1)}, bf16[128,8192]{1,0:T(8,128)(2,1)}, u32[]{:S(2)}) copy-start(bf16[128,8192]{1,0:T(8,128)(2,1)} %token_.3) | copy-start | bytes 6291460
  156.6 40.8 %collective-permute-start.36 = (bf16[128,2048]{1,0:T(8,128)(2,1)S(1)}, bf16[128,2048]{1,0:T(8,128)(2,1)S(1)}, u32[]{:S(2)}, u32[]{:S(2)}) collective-permute-start(bf16[128,2048]{1,0:T(8,128)(2,1)S(1)} %get-tuple-element.150), channel_id=1, source_target_pairs={{0,1},{1,0},{2,3},{3,2},{4,5},{5,4},{6,7},{7,6},{8,9},{9,8},{10,11... | collective-permute-start | bytes 1572872 | tf_op jit(solution)/shard_map/ppermute | solution.py:584
  157.7 39.6 %collective-permute-start.35 = (bf16[128,2048]{1,0:T(8,128)(2,1)S(1)}, bf16[128,2048]{1,0:T(8,128)(2,1)S(1)}, u32[]{:S(2)}, u32[]{:S(2)}) collective-permute-start(bf16[128,2048]{1,0:T(8,128)(2,1)S(1)} %get-tuple-element.151), channel_id=1, source_target_pairs={{0,2},{1,3},{2,0},{3,1},{4,6},{5,7},{6,4},{7,5},{8,10},{9,11},{10,... | collective-permute-start | bytes 1572872 | tf_op jit(solution)/shard_map/ppermute | solution.py:584
  159.3 23.1 %collective-permute-start.32 = (f32[4]{0:T(128)S(1)}, f32[4]{0:T(128)S(1)}, u32[]{:S(2)}, u32[]{:S(2)}) collective-permute-start(f32[4]{0:T(128)S(1)} %add.144), channel_id=1, source_target_pairs={{0,1},{1,0},{2,3},{3,2},{4,5},{5,4},{6,7},{7,6},{8,9},{9,8},{10,11... | collective-permute-start | bytes 56 | tf_op jit(solution)/shard_map/ppermute | solution.py:584
  182.8 16.8 %collective-permute-start.34 = (bf16[128,2048]{1,0:T(8,128)(2,1)S(1)}, bf16[128,2048]{1,0:T(8,128)(2,1)S(1)}, u32[]{:S(2)}, u32[]{:S(2)}) collective-permute-start(bf16[128,2048]{1,0:T(8,128)(2,1)S(1)} %get-tuple-element.148), channel_id=1, source_target_pairs={{0,1},{1,0},{2,3},{3,2},{4,5},{5,4},{6,7},{7,6},{8,9},{9,8},{10,11... | collective-permute-start | bytes 1572872 | tf_op jit(solution)/shard_map/ppermute | solution.py:584
  183.9 15.7 %collective-permute-start.33 = (bf16[128,2048]{1,0:T(8,128)(2,1)S(1)}, bf16[128,2048]{1,0:T(8,128)(2,1)S(1)}, u32[]{:S(2)}, u32[]{:S(2)}) collective-permute-start(bf16[128,2048]{1,0:T(8,128)(2,1)S(1)} %get-tuple-element.149), channel_id=1, source_target_pairs={{0,2},{1,3},{2,0},{3,1},{4,6},{5,7},{6,4},{7,5},{8,10},{9,11},{10,... | collective-permute-start | bytes 1572872 | tf_op jit(solution)/shard_map/ppermute | solution.py:584
  185.5 11.4 %collective-permute-start.37 = (f32[4]{0:T(128)S(1)}, f32[4]{0:T(128)S(1)}, u32[]{:S(2)}, u32[]{:S(2)}) collective-permute-start(f32[4]{0:T(128)S(1)} %add.147), channel_id=1, source_target_pairs={{0,2},{1,3},{2,0},{3,1},{4,6},{5,7},{6,4},{7,5},{8,10},{9,11},{10,... | collective-permute-start | bytes 56 | tf_op jit(solution)/shard_map/ppermute | solution.py:584

commit v3 on v2

--- a/solution.py
+++ b/solution.py
@@ -693,7 +693,7 @@
         totals = all_sum(partial, "tp", n_tp, 1)
         return ((tokens.astype(F32) + mixed).astype(BF16), totals / counts.astype(F32))
 
-    parts = 2
+    parts = 4
     span = half // parts
     sent = []
     for part in range(parts):

time: 205 us -> 216 us (1.054)
  starting transfers between devices: 37.4 us -> 47.1 us
  waiting for transfers between devices: 60.1 us -> 64.1 us
    ppermute x14 -> x22, starting transfers between devices: 16.6 us -> 23.8 us  [flip_tp(): return lax.ppermute(value, 'tp', [(i, i ^ flip) for i in range(n_tp)])]
    ppermute x14 -> x22, waiting for transfers between devices: 40.9 us -> 46.8 us  [flip_tp(): return lax.ppermute(value, 'tp', [(i, i ^ flip) for i in range(n_tp)])]
    ppermute x3, starting transfers between devices: 4.86 us -> 7.52 us  [all_sum(): lax.ppermute(value, axis, [(i, i ^ step) for i in range(size)])]
    pallas_call x2 -> x4, Pallas kernels: 4.85 us -> 5.08 us  [outward(): pl.pallas_call(functools.partial(outward_body, (start, width // 2 + start...]
    pallas_call x2 -> x4, Pallas kernels: 4.47 us -> 4.37 us  [finish(): pl.pallas_call(finish_body, grid=(2, steps), in_specs=specs, out_specs=pl...]
  transfers between devices with their start and end apart: 38 -> 46, of which waited for: 10 -> 15; matrix products, arithmetic and copies ran while one was open for 5% -> 4% of each run, Pallas kernels for 33% -> 32%
where the time goes in v3:
time: 216 us; the launch traced here: 214 us
  Pallas kernels  91.6 us (42%)
  waiting for transfers between devices  64.1 us (30%)
  starting transfers between devices  47.1 us (22%)
  other arithmetic  5.66 us (3%)
  local copies, waits for them, and re-layouts  3.38 us (2%)
    ppermute x22, waiting for transfers between devices, flip_tp(): return lax.ppermute(value, 'tp', [(i, i ^ flip) for i in range(n_tp)])  46.8 us
    ppermute x22, starting transfers between devices, flip_tp(): return lax.ppermute(value, 'tp', [(i, i ^ flip) for i in range(n_tp)])  23.8 us
    pallas_call x1, Pallas kernels, attend(): pl.pallas_call(functools.partial(attend_body, sizes), in_specs=[pl.BlockS...  18 us
    pallas_call x1, Pallas kernels, dequant_joint(): pl.pallas_call(functools.partial(joint_body, len(stored)), in_specs=[pl.B...  17.1 us
    ppermute x9, starting transfers between devices, exchange_along(): lax.ppermute(value, 'ctx', [(i, (i + 2 * step) % n_ctx) for i in range(n_...  13.3 us
    pallas_call x3, Pallas kernels, project_keys(): pl.pallas_call(functools.partial(keys_body, blocks), grid=(1,), in_specs=...  13.1 us
    ppermute x9, waiting for transfers between devices, exchange_along(): lax.ppermute(value, 'ctx', [(i, (i + 2 * step) % n_ctx) for i in range(n_...  11.1 us
    pallas_call x1, Pallas kernels, dequant_back(): pl.pallas_call(back_body, in_specs=[pl.BlockSpec(memory_space=HBM), pl.Bl...  10.3 us
  transfers between devices with their start and end apart: 46, of which 15 were waited for; matrix products, arithmetic and copies ran while one was open for 4% of the time, Pallas kernels for 32%

profile of v3, /device:TPU:0, one launch (start us, length us, event | category | flops | bytes accessed | tf_op | source)
XLA Modules:
  0.0 214.3 jit_solution(11084651831039179706)
XLA Ops:
  0.7 3.0 %collective-permute-start.1 = (bf16[128,8192]{1,0:T(8,128)(2,1)}, bf16[128,8192]{1,0:T(8,128)(2,1)}, u32[]{:S(2)}, u32[]{:S(2)}) collective-permute-start(bf16[128,8192]{1,0:T(8,128)(2,1)} %token_.7), channel_id=1, source_target_pairs={{0,2},{1,3},{2,0},{3,1},{4,6},{5,7},{6,4},{7,5},{8,10},{9,11},{10,... | collective-permute-start | bytes 6291464 | tf_op jit(solution)/shard_map/ppermute | solution.py:584
  3.7 1.5 collective-permute-start
  5.2 0.7 broadcast_in_dim.71
  5.9 0.7 reshape.406
  6.7 0.9 convert_reduce_fusion
  7.7 1.3 dynamic_slice.3
  9.7 1.0 fusion.2
  11.1 0.6 gather_fusion
  12.2 0.7 pad_add_fusion.1.refs_0_
  13.1 0.6 convolution_bitcast_fusion
  13.7 17.1 %shard_map.140.refs_3_.refs_5_.weight = bf16[8192,1536]{1,0:T(8,128)(2,1)S(1)} custom-call(bf16[8192,256]{1,0:T(8,128)(2,1)} %refs_0_.2, bf16[8192,256]{1,0:T(8,128)(2,1)} %refs_1_.2, bf16[8192,1024]{1,0:T(8,128)(2,1)} %refs_2_.1, f32[64,2]{1,0:T(8,128)S(1)} %copy.24.refs_3_, f32[64,2]{1,0:T(8,128)S(1)} %copy.25.refs_4_, f32[64,8]{1,0:T(8,128)S(1)} %copy.26.refs_5_), custom_call_target="tpu_custom_call" | custom-call | flops 7549747200 | bytes 25165824 | tf_op jit(solution)/shard_map/pallas_call | solution.py:135
  30.9 2.9 %shard_map.141 = (bf16[128,8192]{1,0:T(8,128)(2,1)S(1)}, bf16[128,512]{1,0:T(8,128)(2,1)S(1)}) custom-call(bf16[128,8192]{1,0:T(8,128)(2,1)S(1)} %copy-done.1, bf16[128,8192]{1,0:T(8,128)(2,1)S(1)} %copy-done.1, f32[1,8192]{1,0:T(1,128)S(1)} %bitcast.26, bf16[8192,1536]{1,0:T(8,128)(2,1)S(1)} %shard_map.140.refs_3_.refs_5_.weight, ...), custom_call_target="tpu_custom_call" | custom-call | flops 2147483648 | bytes 6291456 | tf_op jit(solution)/shard_map/pallas_call | solution.py:160
  33.9 3.7 %collective-permute-start.4 = (bf16[128,512]{1,0:T(8,128)(2,1)S(1)}, bf16[128,512]{1,0:T(8,128)(2,1)S(1)}, u32[]{:S(2)}, u32[]{:S(2)}) collective-permute-start(bf16[128,512]{1,0:T(8,128)(2,1)S(1)} %get-tuple-element.121.refs_4_), channel_id=1, source_target_pairs={{0,24},{4,28},{8,0},{12,4},{16,8},{20,12},{24,16},{28,20},{1,25},{... | collective-permute-start | bytes 393224 | tf_op jit(solution)/shard_map/ppermute | solution.py:607
  37.5 1.0 collective-permute-start.2
  38.5 2.9 %collective-permute-done.4.refs_7_ = bf16[128,512]{1,0:T(8,128)(2,1)S(1)} collective-permute-done((bf16[128,512]{1,0:T(8,128)(2,1)S(1)}, bf16[128,512]{1,0:T(8,128)(2,1)S(1)}, u32[]{:S(2)}, u32[]{:S(2)}) %collective-permute-start.4) | collective-permute-done | bytes 131104 | tf_op jit(solution)/shard_map/ppermute | solution.py:607
  41.4 8.2 %collective-permute-done.3.refs_6_ = bf16[128,512]{1,0:T(8,128)(2,1)S(1)} collective-permute-done((bf16[128,512]{1,0:T(8,128)(2,1)S(1)}, bf16[128,512]{1,0:T(8,128)(2,1)S(1)}, u32[]{:S(2)}, u32[]{:S(2)}) %collective-permute-start.3) | collective-permute-done | bytes 131104 | tf_op jit(solution)/shard_map/ppermute | solution.py:607
  50.1 2.4 %shard_map.144.refs_1_ = bf16[128,1024]{1,0:T(8,128)(2,1)S(1)} custom-call(bf16[128,8192]{1,0:T(8,128)(2,1)S(1)} %get-tuple-element.104.normed, bf16[8192,1536]{1,0:T(8,128)(2,1)S(1)} %shard_map.140.refs_3_.refs_5_.weight, f32[128,128]{1,0:T(8,128)S(1)} %get-tuple-element.94.refs_4_.cosine, f32[128,128]{1,0:T(8,128)S(1)} %get-tuple-element.95.refs_5_.sine), custom_call_target="tpu_custom_call" | custom-call | flops 4294967296 | bytes 4194304 | tf_op jit(solution)/shard_map/pallas_call | solution.py:183
  52.6 2.4 %shard_map.143 = (bf16[128,4096]{1,0:T(8,128)(2,1)S(1)}, bf16[128,4096]{1,0:T(8,128)(2,1)S(1)}) custom-call(bf16[128,8192]{1,0:T(8,128)(2,1)} %collective-permute-done.refs_0_.refs_1_.one, bf16[128,8192]{1,0:T(8,128)(2,1)} %collective-permute-done.1.refs_2_.refs_3_.two), custom_call_target="tpu_custom_call" | custom-call | bytes 4194304 | tf_op jit(solution)/shard_map/pallas_call | solution.py:271
  55.1 0.6 collective-permute-start.12
  56.2 7.4 %shard_map.142 = (bf16[256,8192]{1,0:T(8,128)(2,1)S(1)}, bf16[256,512]{1,0:T(8,128)(2,1)S(1)}) custom-call(bf16[128,8192]{1,0:T(8,128)(2,1)} %collective-permute-done.refs_0_.refs_1_.one, bf16[128,8192]{1,0:T(8,128)(2,1)} %collective-permute-done.refs_0_.refs_1_.one, bf16[128,8192]{1,0:T(8,128)(2,1)} %collective-permute-done.1.refs_2_.refs_3_.two, ...), custom_call_target="tpu_custom_call" | custom-call | flops 4294967296 | bytes 12582912 | tf_op jit(solution)/shard_map/pallas_call | solution.py:160
  63.6 3.1 %collective-permute-start.11 = (bf16[256,512]{1,0:T(8,128)(2,1)S(1)}, bf16[256,512]{1,0:T(8,128)(2,1)S(1)}, u32[]{:S(2)}, u32[]{:S(2)}) collective-permute-start(bf16[256,512]{1,0:T(8,128)(2,1)S(1)} %get-tuple-element.129.refs_12_), channel_id=1, source_target_pairs={{0,24},{4,28},{8,0},{12,4},{16,8},{20,12},{24,16},{28,20},{1,25},{... | collective-permute-start | bytes 786440 | tf_op jit(solution)/shard_map/ppermute | solution.py:607
  66.7 1.0 collective-permute-start.9
  67.7 4.6 %shard_map.145.refs_2_ = bf16[256,1024]{1,0:T(8,128)(2,1)S(1)} custom-call(bf16[256,8192]{1,0:T(8,128)(2,1)S(1)} %get-tuple-element.105.normed, bf16[8192,1536]{1,0:T(8,128)(2,1)S(1)} %shard_map.140.refs_3_.refs_5_.weight, f32[256,128]{1,0:T(8,128)S(1)} %fusion.1.refs_6_.cosine, f32[256,128]{1,0:T(8,128)S(1)} %fusion.refs_7_.sine), custom_call_target="tpu_custom_call" | custom-call | flops 8589934592 | bytes 8388608 | tf_op jit(solution)/shard_map/pallas_call | solution.py:183
  72.4 7.8 %collective-permute-done.12.refs_0_ = bf16[128,4096]{1,0:T(8,128)(2,1)S(1)} collective-permute-done((bf16[128,4096]{1,0:T(8,128)(2,1)S(1)}, bf16[128,4096]{1,0:T(8,128)(2,1)S(1)}, u32[]{:S(2)}, u32[]{:S(2)}) %collective-permute-start.12) | collective-permute-done | bytes 1048608 | tf_op jit(solution)/shard_map/ppermute | solution.py:584
  80.4 2.8 %shard_map.146 = (bf16[128,8192]{1,0:T(8,128)(2,1)S(1)}, bf16[128,512]{1,0:T(8,128)(2,1)S(1)}) custom-call(bf16[128,4096]{1,0:T(8,128)(2,1)S(1)} %collective-permute-done.12.refs_0_, bf16[128,4096]{1,0:T(8,128)(2,1)S(1)} %collective-permute-done.13.refs_1_, f32[1,8192]{1,0:T(1,128)S(1)} %bitcast.28, ...), custom_call_target="tpu_custom_call" | custom-call | flops 2147483648 | bytes 6291456 | tf_op jit(solution)/shard_map/pallas_call | solution.py:160
  83.2 1.3 collective-permute-start.16
  84.5 1.2 collective-permute-start.15
  85.7 1.9 collective-permute-start.14
  87.7 2.4 %shard_map.147.refs_3_ = bf16[128,1024]{1,0:T(8,128)(2,1)S(1)} custom-call(bf16[128,8192]{1,0:T(8,128)(2,1)S(1)} %get-tuple-element.113.normed, bf16[8192,1536]{1,0:T(8,128)(2,1)S(1)} %shard_map.140.refs_3_.refs_5_.weight, f32[128,128]{1,0:T(8,128)S(1)} %get-tuple-element.108.refs_4_.cosine, f32[128,128]{1,0:T(8,128)S(1)} %get-tuple-element.109.refs_5_.sine), custom_call_target="tpu_custom_call" | custom-call | flops 4294967296 | bytes 4194304 | tf_op jit(solution)/shard_map/pallas_call | solution.py:183
  90.1 10.3 %shard_map.148.weight = bf16[1024,8192]{1,0:T(8,128)(2,1)S(1)} custom-call(bf16[1024,8192]{1,0:T(8,128)(2,1)} %stored.1, f32[8,64]{1,0:T(8,128)S(1)} %copy-done.4), custom_call_target="tpu_custom_call" | custom-call | flops 67108864 | bytes 16777216 | tf_op jit(solution)/shard_map/pallas_call | solution.py:222
  102.6 1.5 collective-permute-done.24.refs_27_
  104.1 18.0 %shard_map.149.attended = bf16[512,1024]{1,0:T(8,128)(2,1)S(1)} custom-call(s32[14]{0:T(128)S(1)} %pad_add_fusion.1.refs_0_, bf16[128,1024]{1,0:T(8,128)(2,1)S(1)} %shard_map.144.refs_1_, bf16[256,1024]{1,0:T(8,128)(2,1)S(1)} %shard_map.145.refs_2_, bf16[128,1024]{1,0:T(8,128)(2,1)S(1)} %shard_map.147.refs_3_, ...), custom_call_target="tpu_custom_call" | custom-call | flops 4294967296 | bytes 8388608 | tf_op jit(solution)/shard_map/pallas_call | solution.py:409
  122.1 1.3 shard_map.150
  123.4 1.1 collective-permute-start.31
  124.6 1.5 collective-permute-start.32
  126.1 1.3 shard_map.151
  127.4 1.0 collective-permute-start.29
  128.9 1.3 shard_map.152
  130.2 1.3 shard_map.153
  131.4 7.2 %shard_map.155 = f32[1024,128]{1,0:T(8,128)S(1)} custom-call(bf16[1024,8192]{1,0:T(8,128)(2,1)S(1)} %shard_map.148.weight, f32[1,8192]{1,0:T(1,128)S(1)} %bitcast.29), custom_call_target="tpu_custom_call" | custom-call | flops 67108864 | bytes 16777216 | tf_op jit(solution)/shard_map/pallas_call | solution.py:250
  138.6 4.5 %shard_map.154 = (bf16[128,8192]{1,0:T(8,128)(2,1)S(1)}, bf16[128,8192]{1,0:T(8,128)(2,1)S(1)}) custom-call(bf16[512,1024]{1,0:T(8,128)(2,1)S(1)} %shard_map.149.attended, bf16[1024,8192]{1,0:T(8,128)(2,1)S(1)} %shard_map.148.weight), custom_call_target="tpu_custom_call" | custom-call | flops 8589934592 | bytes 4194304 | tf_op jit(solution)/shard_map/pallas_call | solution.py:480
  143.8 1.1 collective-permute-done.33
  145.0 1.7 collective-permute-start.34
  146.6 1.9 collective-permute-done.34
  148.5 5.8 %collective-permute-start.35 = (f32[4]{0:T(128)S(1)}, f32[4]{0:T(128)S(1)}, u32[]{:S(2)}, u32[]{:S(2)}) collective-permute-start(f32[4]{0:T(128)S(1)} %add.155), channel_id=1, source_target_pairs={{0,16},{4,20},{8,24},{12,28},{16,0},{20,4},{24,8},{28,12},{1,17},{... | collective-permute-start | bytes 56 | tf_op jit(solution)/shard_map/ppermute | solution.py:677
  154.3 1.5 collective-permute-done.35
  156.3 1.5 collective-permute-start.28
  157.9 1.5 collective-permute-start.25
  159.6 0.6 collective-permute-start.36
  160.2 19.2 %collective-permute-done.36 = f32[4]{0:T(128)S(1)} collective-permute-done((f32[4]{0:T(128)S(1)}, f32[4]{0:T(128)S(1)}, u32[]{:S(2)}, u32[]{:S(2)}) %collective-permute-start.36) | collective-permute-done | bytes 48 | tf_op jit(solution)/shard_map/ppermute | solution.py:584
  179.4 1.5 collective-permute-start.26
  181.7 9.6 %collective-permute-done.37 = f32[4]{0:T(128)S(1)} collective-permute-done((f32[4]{0:T(128)S(1)}, f32[4]{0:T(128)S(1)}, u32[]{:S(2)}, u32[]{:S(2)}) %collective-permute-start.37) | collective-permute-done | bytes 48 | tf_op jit(solution)/shard_map/ppermute | solution.py:584
  191.3 1.6 collective-permute-start.44
  192.9 2.0 collective-permute-start.43
  195.9 4.6 %collective-permute-done.45.far_x = bf16[128,1024]{1,0:T(8,128)(2,1)S(1)} collective-permute-done((bf16[128,1024]{1,0:T(8,128)(2,1)S(1)}, bf16[128,1024]{1,0:T(8,128)(2,1)S(1)}, u32[]{:S(2)}, u32[]{:S(2)}) %collective-permute-start.45) | collective-permute-done | bytes 262176 | tf_op jit(solution)/shard_map/ppermute | solution.py:584
  200.5 1.5 collective-permute-start.40
  202.6 3.6 %collective-permute-done.43.far_x = bf16[128,1024]{1,0:T(8,128)(2,1)S(1)} collective-permute-done((bf16[128,1024]{1,0:T(8,128)(2,1)S(1)}, bf16[128,1024]{1,0:T(8,128)(2,1)S(1)}, u32[]{:S(2)}, u32[]{:S(2)}) %collective-permute-start.43) | collective-permute-done | bytes 262176 | tf_op jit(solution)/shard_map/ppermute | solution.py:584
  206.1 1.5 collective-permute-start.38
  208.2 1.1 shard_map.156.rest_0_
  209.3 1.1 shard_map.157.rest_0_
  210.4 1.1 shard_map.158.rest_0_
  211.5 0.8 collective-permute-done.39.far_x
  212.3 0.9 collective-permute-done.38.far_y
  213.2 1.1 shard_map.159
  (105 shorter events, 9.5 us)
Async XLA Ops:
  0.6 12.5 %copy-start = (bf16[128,8192]{1,0:T(8,128)(2,1)S(1)}, bf16[128,8192]{1,0:T(8,128)(2,1)}, u32[]{:S(2)}) copy-start(bf16[128,8192]{1,0:T(8,128)(2,1)} %token_.7) | copy-start | bytes 6291460
  0.6 10.5 %copy-start.5 = (s32[8]{0:T(128)S(1)}, s32[8]{0:T(128)}, u32[]{:S(2)}) copy-start(s32[8]{0:T(128)} %param.25) | copy-start | bytes 100
  0.7 11.1 %copy-start.6 = (f32[64,8]{0,1:T(8,128)S(1)}, f32[64,8]{0,1:T(8,128)}, u32[]{:S(2)}) copy-start(f32[64,8]{0,1:T(8,128)} %param.16) | copy-start | bytes 6148
  0.7 11.2 %copy-start.7 = (f32[64,2]{0,1:T(2,128)S(1)}, f32[64,2]{0,1:T(2,128)}, u32[]{:S(2)}) copy-start(f32[64,2]{0,1:T(2,128)} %param.18) | copy-start | bytes 1540
  0.7 11.3 %copy-start.8 = (f32[64,2]{0,1:T(2,128)S(1)}, f32[64,2]{0,1:T(2,128)}, u32[]{:S(2)}) copy-start(f32[64,2]{0,1:T(2,128)} %param.20) | copy-start | bytes 1540
  0.7 51.9 %collective-permute-start.1 = (bf16[128,8192]{1,0:T(8,128)(2,1)}, bf16[128,8192]{1,0:T(8,128)(2,1)}, u32[]{:S(2)}, u32[]{:S(2)}) collective-permute-start(bf16[128,8192]{1,0:T(8,128)(2,1)} %token_.7), channel_id=1, source_target_pairs={{0,2},{1,3},{2,0},{3,1},{4,6},{5,7},{6,4},{7,5},{8,10},{9,11},{10,... | collective-permute-start | bytes 6291464 | tf_op jit(solution)/shard_map/ppermute | solution.py:584
  3.7 48.9 %collective-permute-start = (bf16[128,8192]{1,0:T(8,128)(2,1)}, bf16[128,8192]{1,0:T(8,128)(2,1)}, u32[]{:S(2)}, u32[]{:S(2)}) collective-permute-start(bf16[128,8192]{1,0:T(8,128)(2,1)} %token_.7), channel_id=1, source_target_pairs={{0,1},{1,0},{2,3},{3,2},{4,5},{5,4},{6,7},{7,6},{8,9},{9,8},{10,11... | collective-permute-start | bytes 6291464 | tf_op jit(solution)/shard_map/ppermute | solution.py:584
  13.7 17.1 %copy-start.1 = (bf16[128,8192]{1,0:T(8,128)(2,1)S(1)}, bf16[128,8192]{1,0:T(8,128)(2,1)}, u32[]{:S(2)}) copy-start(bf16[128,8192]{1,0:T(8,128)(2,1)} %token_.7) | copy-start | bytes 6291460
  13.7 17.1 %copy-start.3 = (f32[8192]{0:T(1024)S(1)}, f32[8192]{0:T(1024)}, u32[]{:S(2)}) copy-start(f32[8192]{0:T(1024)} %param.14) | copy-start | bytes 98308
  33.8 3.7 %collective-permute-start.5 = (bf16[128,512]{1,0:T(8,128)(2,1)S(1)}, bf16[128,512]{1,0:T(8,128)(2,1)S(1)}, u32[]{:S(2)}, u32[]{:S(2)}) collective-permute-start(bf16[128,512]{1,0:T(8,128)(2,1)S(1)} %get-tuple-element.121.refs_4_), channel_id=1, source_target_pairs={{0,4},{4,0},{8,12},{12,8},{16,20},{20,16},{24,28},{28,24},{1,5},{5... | collective-permute-start | bytes 393224 | tf_op jit(solution)/shard_map/ppermute | solution.py:613
  33.9 7.6 %collective-permute-start.4 = (bf16[128,512]{1,0:T(8,128)(2,1)S(1)}, bf16[128,512]{1,0:T(8,128)(2,1)S(1)}, u32[]{:S(2)}, u32[]{:S(2)}) collective-permute-start(bf16[128,512]{1,0:T(8,128)(2,1)S(1)} %get-tuple-element.121.refs_4_), channel_id=1, source_target_pairs={{0,24},{4,28},{8,0},{12,4},{16,8},{20,12},{24,16},{28,20},{1,25},{... | collective-permute-start | bytes 393224 | tf_op jit(solution)/shard_map/ppermute | solution.py:607
  37.5 12.1 %collective-permute-start.3 = (bf16[128,512]{1,0:T(8,128)(2,1)S(1)}, bf16[128,512]{1,0:T(8,128)(2,1)S(1)}, u32[]{:S(2)}, u32[]{:S(2)}) collective-permute-start(bf16[128,512]{1,0:T(8,128)(2,1)S(1)} %get-tuple-element.121.refs_4_), channel_id=1, source_target_pairs={{0,16},{4,20},{8,24},{12,28},{16,0},{20,4},{24,8},{28,12},{1,17},{... | collective-permute-start | bytes 393224 | tf_op jit(solution)/shard_map/ppermute | solution.py:607
  37.5 12.1 %collective-permute-start.2 = (bf16[128,512]{1,0:T(8,128)(2,1)S(1)}, bf16[128,512]{1,0:T(8,128)(2,1)S(1)}, u32[]{:S(2)}, u32[]{:S(2)}) collective-permute-start(bf16[128,512]{1,0:T(8,128)(2,1)S(1)} %get-tuple-element.121.refs_4_), channel_id=1, source_target_pairs={{0,8},{4,12},{8,16},{12,20},{16,24},{20,28},{24,0},{28,4},{1,9},{5... | collective-permute-start | bytes 393224 | tf_op jit(solution)/shard_map/ppermute | solution.py:607
  41.4 11.1 %collective-permute-start.8 = (bf16[128,512]{1,0:T(8,128)(2,1)S(1)}, bf16[128,512]{1,0:T(8,128)(2,1)S(1)}, u32[]{:S(2)}, u32[]{:S(2)}) collective-permute-start(bf16[128,512]{1,0:T(8,128)(2,1)S(1)} %collective-permute-done.4.refs_7_), channel_id=1, source_target_pairs={{0,4},{4,0},{8,12},{12,8},{16,20},{20,16},{24,28},{28,24},{1,5},{5... | collective-permute-start | bytes 393224 | tf_op jit(solution)/shard_map/ppermute | solution.py:613
  49.6 3.0 %collective-permute-start.7 = (bf16[128,512]{1,0:T(8,128)(2,1)S(1)}, bf16[128,512]{1,0:T(8,128)(2,1)S(1)}, u32[]{:S(2)}, u32[]{:S(2)}) collective-permute-start(bf16[128,512]{1,0:T(8,128)(2,1)S(1)} %collective-permute-done.3.refs_6_), channel_id=1, source_target_pairs={{0,4},{4,0},{8,12},{12,8},{16,20},{20,16},{24,28},{28,24},{1,5},{5... | collective-permute-start | bytes 393224 | tf_op jit(solution)/shard_map/ppermute | solution.py:613
  49.6 3.0 %collective-permute-start.6 = (bf16[128,512]{1,0:T(8,128)(2,1)S(1)}, bf16[128,512]{1,0:T(8,128)(2,1)S(1)}, u32[]{:S(2)}, u32[]{:S(2)}) collective-permute-start(bf16[128,512]{1,0:T(8,128)(2,1)S(1)} %collective-permute-done.2.refs_5_), channel_id=1, source_target_pairs={{0,4},{4,0},{8,12},{12,8},{16,20},{20,16},{24,28},{28,24},{1,5},{5... | collective-permute-start | bytes 393224 | tf_op jit(solution)/shard_map/ppermute | solution.py:613
  55.1 25.1 %collective-permute-start.12 = (bf16[128,4096]{1,0:T(8,128)(2,1)S(1)}, bf16[128,4096]{1,0:T(8,128)(2,1)S(1)}, u32[]{:S(2)}, u32[]{:S(2)}) collective-permute-start(bf16[128,4096]{1,0:T(8,128)(2,1)S(1)} %get-tuple-element.102), channel_id=1, source_target_pairs={{0,2},{1,3},{2,0},{3,1},{4,6},{5,7},{6,4},{7,5},{8,10},{9,11},{10,... | collective-permute-start | bytes 3145736 | tf_op jit(solution)/shard_map/ppermute | solution.py:584
  55.6 24.8 %collective-permute-start.13 = (bf16[128,4096]{1,0:T(8,128)(2,1)S(1)}, bf16[128,4096]{1,0:T(8,128)(2,1)S(1)}, u32[]{:S(2)}, u32[]{:S(2)}) collective-permute-start(bf16[128,4096]{1,0:T(8,128)(2,1)S(1)} %get-tuple-element.103), channel_id=1, source_target_pairs={{0,1},{1,0},{2,3},{3,2},{4,5},{5,4},{6,7},{7,6},{8,9},{9,8},{10,11... | collective-permute-start | bytes 3145736 | tf_op jit(solution)/shard_map/ppermute | solution.py:584
  63.6 22.1 %collective-permute-start.11 = (bf16[256,512]{1,0:T(8,128)(2,1)S(1)}, bf16[256,512]{1,0:T(8,128)(2,1)S(1)}, u32[]{:S(2)}, u32[]{:S(2)}) collective-permute-start(bf16[256,512]{1,0:T(8,128)(2,1)S(1)} %get-tuple-element.129.refs_12_), channel_id=1, source_target_pairs={{0,24},{4,28},{8,0},{12,4},{16,8},{20,12},{24,16},{28,20},{1,25},{... | collective-permute-start | bytes 786440 | tf_op jit(solution)/shard_map/ppermute | solution.py:607
  66.7 33.7 %collective-permute-start.10 = (bf16[256,512]{1,0:T(8,128)(2,1)S(1)}, bf16[256,512]{1,0:T(8,128)(2,1)S(1)}, u32[]{:S(2)}, u32[]{:S(2)}) collective-permute-start(bf16[256,512]{1,0:T(8,128)(2,1)S(1)} %get-tuple-element.129.refs_12_), channel_id=1, source_target_pairs={{0,16},{4,20},{8,24},{12,28},{16,0},{20,4},{24,8},{28,12},{1,17},{... | collective-permute-start | bytes 786440 | tf_op jit(solution)/shard_map/ppermute | solution.py:607
  66.7 33.7 %collective-permute-start.9 = (bf16[256,512]{1,0:T(8,128)(2,1)S(1)}, bf16[256,512]{1,0:T(8,128)(2,1)S(1)}, u32[]{:S(2)}, u32[]{:S(2)}) collective-permute-start(bf16[256,512]{1,0:T(8,128)(2,1)S(1)} %get-tuple-element.129.refs_12_), channel_id=1, source_target_pairs={{0,8},{4,12},{8,16},{12,20},{16,24},{20,28},{24,0},{28,4},{1,9},{5... | collective-permute-start | bytes 786440 | tf_op jit(solution)/shard_map/ppermute | solution.py:607
  83.2 17.2 %collective-permute-start.16 = (bf16[128,512]{1,0:T(8,128)(2,1)S(1)}, bf16[128,512]{1,0:T(8,128)(2,1)S(1)}, u32[]{:S(2)}, u32[]{:S(2)}) collective-permute-start(bf16[128,512]{1,0:T(8,128)(2,1)S(1)} %get-tuple-element.133.refs_20_), channel_id=1, source_target_pairs={{0,24},{4,28},{8,0},{12,4},{16,8},{20,12},{24,16},{28,20},{1,25},{... | collective-permute-start | bytes 393224 | tf_op jit(solution)/shard_map/ppermute | solution.py:607
  84.5 15.9 %collective-permute-start.15 = (bf16[128,512]{1,0:T(8,128)(2,1)S(1)}, bf16[128,512]{1,0:T(8,128)(2,1)S(1)}, u32[]{:S(2)}, u32[]{:S(2)}) collective-permute-start(bf16[128,512]{1,0:T(8,128)(2,1)S(1)} %get-tuple-element.133.refs_20_), channel_id=1, source_target_pairs={{0,16},{4,20},{8,24},{12,28},{16,0},{20,4},{24,8},{28,12},{1,17},{... | collective-permute-start | bytes 393224 | tf_op jit(solution)/shard_map/ppermute | solution.py:607
  85.7 14.7 %collective-permute-start.14 = (bf16[128,512]{1,0:T(8,128)(2,1)S(1)}, bf16[128,512]{1,0:T(8,128)(2,1)S(1)}, u32[]{:S(2)}, u32[]{:S(2)}) collective-permute-start(bf16[128,512]{1,0:T(8,128)(2,1)S(1)} %get-tuple-element.133.refs_20_), channel_id=1, source_target_pairs={{0,8},{4,12},{8,16},{12,20},{16,24},{20,28},{24,0},{28,4},{1,9},{5... | collective-permute-start | bytes 393224 | tf_op jit(solution)/shard_map/ppermute | solution.py:607
  87.7 2.5 %copy-start.4 = (f32[8,64]{1,0:T(8,128)S(1)}, f32[8,64]{1,0:T(8,128)}, u32[]{:S(2)}) copy-start(f32[8,64]{1,0:T(8,128)} %scales) | copy-start | bytes 6148
  100.5 1.4 collective-permute-start.21
  100.5 1.5 collective-permute-start.22
  101.0 1.4 collective-permute-start.23
  101.1 3.0 %collective-permute-start.17 = (bf16[256,512]{1,0:T(8,128)(2,1)S(1)}, bf16[256,512]{1,0:T(8,128)(2,1)S(1)}, u32[]{:S(2)}, u32[]{:S(2)}) collective-permute-start(bf16[256,512]{1,0:T(8,128)(2,1)S(1)} %get-tuple-element.129.refs_12_), channel_id=1, source_target_pairs={{0,4},{4,0},{8,12},{12,8},{16,20},{20,16},{24,28},{28,24},{1,5},{5... | collective-permute-start | bytes 786440 | tf_op jit(solution)/shard_map/ppermute | solution.py:613
  101.5 2.5 %collective-permute-start.18 = (bf16[256,512]{1,0:T(8,128)(2,1)S(1)}, bf16[256,512]{1,0:T(8,128)(2,1)S(1)}, u32[]{:S(2)}, u32[]{:S(2)}) collective-permute-start(bf16[256,512]{1,0:T(8,128)(2,1)S(1)} %collective-permute-done.9.refs_13_), channel_id=1, source_target_pairs={{0,4},{4,0},{8,12},{12,8},{16,20},{20,16},{24,28},{28,24},{1,5},{5... | collective-permute-start | bytes 786440 | tf_op jit(solution)/shard_map/ppermute | solution.py:613
  101.9 2.2 %collective-permute-start.19 = (bf16[256,512]{1,0:T(8,128)(2,1)S(1)}, bf16[256,512]{1,0:T(8,128)(2,1)S(1)}, u32[]{:S(2)}, u32[]{:S(2)}) collective-permute-start(bf16[256,512]{1,0:T(8,128)(2,1)S(1)} %collective-permute-done.10.refs_14_), channel_id=1, source_target_pairs={{0,4},{4,0},{8,12},{12,8},{16,20},{20,16},{24,28},{28,24},{1,5},{5... | collective-permute-start | bytes 786440 | tf_op jit(solution)/shard_map/ppermute | solution.py:613
  102.1 2.0 collective-permute-start.20
  102.4 1.7 collective-permute-start.24
  123.4 32.9 %collective-permute-start.31 = (bf16[256,1024]{1,0:T(8,128)(2,1)S(1)}, bf16[256,1024]{1,0:T(8,128)(2,1)S(1)}, u32[]{:S(2)}, u32[]{:S(2)}) collective-permute-start(bf16[256,1024]{1,0:T(8,128)(2,1)S(1)} %get-tuple-element.139), channel_id=1, source_target_pairs={{0,1},{1,0},{2,3},{3,2},{4,5},{5,4},{6,7},{7,6},{8,9},{9,8},{10,11... | collective-permute-start | bytes 1572872 | tf_op jit(solution)/shard_map/ppermute | solution.py:584
  124.6 33.3 %collective-permute-start.32 = (bf16[256,1024]{1,0:T(8,128)(2,1)S(1)}, bf16[256,1024]{1,0:T(8,128)(2,1)S(1)}, u32[]{:S(2)}, u32[]{:S(2)}) collective-permute-start(bf16[256,1024]{1,0:T(8,128)(2,1)S(1)} %get-tuple-element.140), channel_id=1, source_target_pairs={{0,2},{1,3},{2,0},{3,1},{4,6},{5,7},{6,4},{7,5},{8,10},{9,11},{10,... | collective-permute-start | bytes 1572872 | tf_op jit(solution)/shard_map/ppermute | solution.py:584
  127.4 32.2 %collective-permute-start.29 = (bf16[256,1024]{1,0:T(8,128)(2,1)S(1)}, bf16[256,1024]{1,0:T(8,128)(2,1)S(1)}, u32[]{:S(2)}, u32[]{:S(2)}) collective-permute-start(bf16[256,1024]{1,0:T(8,128)(2,1)S(1)} %get-tuple-element.143), channel_id=1, source_target_pairs={{0,1},{1,0},{2,3},{3,2},{4,5},{5,4},{6,7},{7,6},{8,9},{9,8},{10,11... | collective-permute-start | bytes 1572872 | tf_op jit(solution)/shard_map/ppermute | solution.py:584
  128.4 52.6 %collective-permute-start.30 = (bf16[256,1024]{1,0:T(8,128)(2,1)S(1)}, bf16[256,1024]{1,0:T(8,128)(2,1)S(1)}, u32[]{:S(2)}, u32[]{:S(2)}) collective-permute-start(bf16[256,1024]{1,0:T(8,128)(2,1)S(1)} %get-tuple-element.144), channel_id=1, source_target_pairs={{0,2},{1,3},{2,0},{3,1},{4,6},{5,7},{6,4},{7,5},{8,10},{9,11},{10,... | collective-permute-start | bytes 1572872 | tf_op jit(solution)/shard_map/ppermute | solution.py:584
  143.8 1.2 collective-permute-start.33
  145.0 3.5 %collective-permute-start.34 = (f32[4]{0:T(128)S(1)}, f32[4]{0:T(128)S(1)}, u32[]{:S(2)}, u32[]{:S(2)}) collective-permute-start(f32[4]{0:T(128)S(1)} %add.154), channel_id=1, source_target_pairs={{0,8},{4,12},{8,0},{12,4},{16,24},{20,28},{24,16},{28,20},{1,9},{5... | collective-permute-start | bytes 56 | tf_op jit(solution)/shard_map/ppermute | solution.py:677
  148.5 7.3 %collective-permute-start.35 = (f32[4]{0:T(128)S(1)}, f32[4]{0:T(128)S(1)}, u32[]{:S(2)}, u32[]{:S(2)}) collective-permute-start(f32[4]{0:T(128)S(1)} %add.155), channel_id=1, source_target_pairs={{0,16},{4,20},{8,24},{12,28},{16,0},{20,4},{24,8},{28,12},{1,17},{... | collective-permute-start | bytes 56 | tf_op jit(solution)/shard_map/ppermute | solution.py:677
  155.8 35.5 %collective-permute-start.27 = (bf16[256,1024]{1,0:T(8,128)(2,1)S(1)}, bf16[256,1024]{1,0:T(8,128)(2,1)S(1)}, u32[]{:S(2)}, u32[]{:S(2)}) collective-permute-start(bf16[256,1024]{1,0:T(8,128)(2,1)S(1)} %get-tuple-element.147), channel_id=1, source_target_pairs={{0,1},{1,0},{2,3},{3,2},{4,5},{5,4},{6,7},{7,6},{8,9},{9,8},{10,11... | collective-permute-start | bytes 1572872 | tf_op jit(solution)/shard_map/ppermute | solution.py:584
  156.3 36.5 %collective-permute-start.28 = (bf16[256,1024]{1,0:T(8,128)(2,1)S(1)}, bf16[256,1024]{1,0:T(8,128)(2,1)S(1)}, u32[]{:S(2)}, u32[]{:S(2)}) collective-permute-start(bf16[256,1024]{1,0:T(8,128)(2,1)S(1)} %get-tuple-element.148), channel_id=1, source_target_pairs={{0,2},{1,3},{2,0},{3,1},{4,6},{5,7},{6,4},{7,5},{8,10},{9,11},{10,... | collective-permute-start | bytes 1572872 | tf_op jit(solution)/shard_map/ppermute | solution.py:584
  157.9 37.2 %collective-permute-start.25 = (bf16[256,1024]{1,0:T(8,128)(2,1)S(1)}, bf16[256,1024]{1,0:T(8,128)(2,1)S(1)}, u32[]{:S(2)}, u32[]{:S(2)}) collective-permute-start(bf16[256,1024]{1,0:T(8,128)(2,1)S(1)} %get-tuple-element.150), channel_id=1, source_target_pairs={{0,1},{1,0},{2,3},{3,2},{4,5},{5,4},{6,7},{7,6},{8,9},{9,8},{10,11... | collective-permute-start | bytes 1572872 | tf_op jit(solution)/shard_map/ppermute | solution.py:584
  159.6 19.8 %collective-permute-start.36 = (f32[4]{0:T(128)S(1)}, f32[4]{0:T(128)S(1)}, u32[]{:S(2)}, u32[]{:S(2)}) collective-permute-start(f32[4]{0:T(128)S(1)} %add.156), channel_id=1, source_target_pairs={{0,1},{1,0},{2,3},{3,2},{4,5},{5,4},{6,7},{7,6},{8,9},{9,8},{10,11... | collective-permute-start | bytes 56 | tf_op jit(solution)/shard_map/ppermute | solution.py:584
  179.4 16.2 %collective-permute-start.26 = (bf16[256,1024]{1,0:T(8,128)(2,1)S(1)}, bf16[256,1024]{1,0:T(8,128)(2,1)S(1)}, u32[]{:S(2)}, u32[]{:S(2)}) collective-permute-start(bf16[256,1024]{1,0:T(8,128)(2,1)S(1)} %get-tuple-element.151), channel_id=1, source_target_pairs={{0,2},{1,3},{2,0},{3,1},{4,6},{5,7},{6,4},{7,5},{8,10},{9,11},{10,... | collective-permute-start | bytes 1572872 | tf_op jit(solution)/shard_map/ppermute | solution.py:584
  180.9 27.3 %copy-start.2 = (bf16[128,8192]{1,0:T(8,128)(2,1)S(1)}, bf16[128,8192]{1,0:T(8,128)(2,1)}, u32[]{:S(2)}) copy-start(bf16[128,8192]{1,0:T(8,128)(2,1)} %token_.7) | copy-start | bytes 6291460
  181.1 10.2 %collective-permute-start.37 = (f32[4]{0:T(128)S(1)}, f32[4]{0:T(128)S(1)}, u32[]{:S(2)}, u32[]{:S(2)}) collective-permute-start(f32[4]{0:T(128)S(1)} %add.159), channel_id=1, source_target_pairs={{0,2},{1,3},{2,0},{3,1},{4,6},{5,7},{6,4},{7,5},{8,10},{9,11},{10,... | collective-permute-start | bytes 56 | tf_op jit(solution)/shard_map/ppermute | solution.py:584
  191.3 9.2 %collective-permute-start.45 = (bf16[128,1024]{1,0:T(8,128)(2,1)S(1)}, bf16[128,1024]{1,0:T(8,128)(2,1)S(1)}, u32[]{:S(2)}, u32[]{:S(2)}) collective-permute-start(bf16[128,1024]{1,0:T(8,128)(2,1)S(1)} %get-tuple-element.190), channel_id=1, source_target_pairs={{0,1},{1,0},{2,3},{3,2},{4,5},{5,4},{6,7},{7,6},{8,9},{9,8},{10,11... | collective-permute-start | bytes 786440 | tf_op jit(solution)/shard_map/ppermute | solution.py:584
  191.3 10.7 %collective-permute-start.44 = (bf16[128,1024]{1,0:T(8,128)(2,1)S(1)}, bf16[128,1024]{1,0:T(8,128)(2,1)S(1)}, u32[]{:S(2)}, u32[]{:S(2)}) collective-permute-start(bf16[128,1024]{1,0:T(8,128)(2,1)S(1)} %get-tuple-element.191), channel_id=1, source_target_pairs={{0,2},{1,3},{2,0},{3,1},{4,6},{5,7},{6,4},{7,5},{8,10},{9,11},{10,... | collective-permute-start | bytes 786440 | tf_op jit(solution)/shard_map/ppermute | solution.py:584
  192.9 13.3 %collective-permute-start.43 = (bf16[128,1024]{1,0:T(8,128)(2,1)S(1)}, bf16[128,1024]{1,0:T(8,128)(2,1)S(1)}, u32[]{:S(2)}, u32[]{:S(2)}) collective-permute-start(bf16[128,1024]{1,0:T(8,128)(2,1)S(1)} %get-tuple-element.188), channel_id=1, source_target_pairs={{0,1},{1,0},{2,3},{3,2},{4,5},{5,4},{6,7},{7,6},{8,9},{9,8},{10,11... | collective-permute-start | bytes 786440 | tf_op jit(solution)/shard_map/ppermute | solution.py:584
  195.1 14.2 %collective-permute-start.42 = (bf16[128,1024]{1,0:T(8,128)(2,1)S(1)}, bf16[128,1024]{1,0:T(8,128)(2,1)S(1)}, u32[]{:S(2)}, u32[]{:S(2)}) collective-permute-start(bf16[128,1024]{1,0:T(8,128)(2,1)S(1)} %get-tuple-element.189), channel_id=1, source_target_pairs={{0,2},{1,3},{2,0},{3,1},{4,6},{5,7},{6,4},{7,5},{8,10},{9,11},{10,... | collective-permute-start | bytes 786440 | tf_op jit(solution)/shard_map/ppermute | solution.py:584
  195.6 14.8 %collective-permute-start.41 = (bf16[128,1024]{1,0:T(8,128)(2,1)S(1)}, bf16[128,1024]{1,0:T(8,128)(2,1)S(1)}, u32[]{:S(2)}, u32[]{:S(2)}) collective-permute-start(bf16[128,1024]{1,0:T(8,128)(2,1)S(1)} %get-tuple-element.184), channel_id=1, source_target_pairs={{0,1},{1,0},{2,3},{3,2},{4,5},{5,4},{6,7},{7,6},{8,9},{9,8},{10,11... | collective-permute-start | bytes 786440 | tf_op jit(solution)/shard_map/ppermute | solution.py:584
  200.5 9.9 %collective-permute-start.40 = (bf16[128,1024]{1,0:T(8,128)(2,1)S(1)}, bf16[128,1024]{1,0:T(8,128)(2,1)S(1)}, u32[]{:S(2)}, u32[]{:S(2)}) collective-permute-start(bf16[128,1024]{1,0:T(8,128)(2,1)S(1)} %get-tuple-element.185), channel_id=1, source_target_pairs={{0,2},{1,3},{2,0},{3,1},{4,6},{5,7},{6,4},{7,5},{8,10},{9,11},{10,... | collective-permute-start | bytes 786440 | tf_op jit(solution)/shard_map/ppermute | solution.py:584
  202.1 10.3 %collective-permute-start.39 = (bf16[128,1024]{1,0:T(8,128)(2,1)S(1)}, bf16[128,1024]{1,0:T(8,128)(2,1)S(1)}, u32[]{:S(2)}, u32[]{:S(2)}) collective-permute-start(bf16[128,1024]{1,0:T(8,128)(2,1)S(1)} %get-tuple-element.186), channel_id=1, source_target_pairs={{0,1},{1,0},{2,3},{3,2},{4,5},{5,4},{6,7},{7,6},{8,9},{9,8},{10,11... | collective-permute-start | bytes 786440 | tf_op jit(solution)/shard_map/ppermute | solution.py:584
  206.1 7.0 %collective-permute-start.38 = (bf16[128,1024]{1,0:T(8,128)(2,1)S(1)}, bf16[128,1024]{1,0:T(8,128)(2,1)S(1)}, u32[]{:S(2)}, u32[]{:S(2)}) collective-permute-start(bf16[128,1024]{1,0:T(8,128)(2,1)S(1)} %get-tuple-element.187), channel_id=1, source_target_pairs={{0,2},{1,3},{2,0},{3,1},{4,6},{5,7},{6,4},{7,5},{8,10},{9,11},{10,... | collective-permute-start | bytes 786440 | tf_op jit(solution)/shard_map/ppermute | solution.py:584
